TPU v7x, 32 devices: a whole 2x2x4 slice. The times are simulated.
32 devices in a mesh: grp: 2 (over x), tile: 16 (over z, y, core).
Axes of the slice: x: 2, y: 2, z: 4, core: 2. Of those that a mesh axis runs over, the one named last changes fastest.
Arguments:
- prognostic: float32 [4, 64, 256, 256], P(None, None, 'tile'), may hold values from 0.2 to 2
- courant: float32 [2, 64, 256, 256], P(None, None, 'tile'), may hold values from -0.22 to 0.22
- daylit: int32 [16384], P('tile'), may hold values from 0 to 1, as said below
- cos_zenith: float32 [16384], P('tile'), may hold values from 0.05 to 1
- albedo: float32 [16384], P('tile'), may hold values from 0.05 to 0.8
- layer_mass: float32 [64], replicated, may hold values from 0.5 to 2
- vapour_absorption: float32 [64, 32], replicated, may hold values from 0.002 to 0.1
- ozone_absorption: float32 [32], replicated, may hold values from 0.002 to 0.1
- cloud_extinction: float32 [32], replicated, may hold values from 0.005 to 0.1
- cloud_albedo: float32 [32], replicated, may hold values from 0.5 to 0.95
- solar_weight: float32 [32], replicated, may hold values from 0.01 to 0.06
Outputs:
- stepped: float32 [2, 4, 64, 256, 256], P('grp', None, None, 'tile')
Inputs may be any that keep to these rules, and one draw needn't show every extreme that they name: In all, exactly 8192 coarse columns are daylit.
All inputs are finite; a program needn't handle non-finite values.
Results may differ from a plain program's by a relative error of at most 0.00002.
Values sent between devices are 32-bit elements; how exact they have to be, the bound alone decides.
A program may use at most 256 MiB of HBM per device.

v0:
```python
import functools

import jax
import jax.numpy as jnp
from jax import lax
from jax.experimental import pallas as pl
from jax.experimental.pallas import tpu as pltpu
from jax.sharding import PartitionSpec as P

COARSEN = 4
DIFFUSIVITY = 1.66
STEP_LENGTH = 1.0
LOG2E = 1.4426950408889634
G_CHUNK = 8
LEVEL_BLOCK = 8
VMEM_LIMIT = 56 * 1024 * 1024


def pack_means(tile):
    sub = lax.broadcasted_iota(jnp.int32, (8, 128), 0) % 4
    packed = None
    for xh in range(2):
        for yh in range(2):
            part = tile[8 * xh : 8 * xh + 8, 128 * yh : 128 * yh + 128]
            part = part + pltpu.roll(part, 7, 0)
            part = part + pltpu.roll(part, 6, 0)
            k = 2 * xh + yh
            if k:
                part = pltpu.roll(part, k, 0)
            packed = part if packed is None else jnp.where(sub == k, part, packed)
    return packed * (1.0 / COARSEN)


def spread_part(packed, xh, yh):
    k = 2 * xh + yh
    low = jnp.broadcast_to(packed[k : k + 1], (8, 128))
    high = jnp.broadcast_to(packed[4 + k : 5 + k], (8, 128))
    return jnp.where(lax.broadcasted_iota(jnp.int32, (8, 128), 0) < 4, low, high)


def register_order(rows):
    return jnp.concatenate([rows[0:2], rows[4:6], rows[2:4], rows[6:8]], axis=0)


def radiation_kernel(
    mass_s, vap_s, oz_s, ext_s, alb_s, sol_s,
    lit_ref, cos_ref, ground_ref, prog_ref,
    out_ref, heat_ref,
    coarse, acc, k_tdir, k_a, k_b, k_ad, k_as,
):
    chunk = pl.program_id(0)
    levels = prog_ref.shape[1]

    @pl.when(chunk == 0)
    def _():
        def body(l, c):
            scale = mass_s[l]
            for f in range(3):
                coarse[f, l] = pack_means(prog_ref[f + 1, l]) * scale
            for f in range(4):
                acc[f, l] = jnp.zeros((8, 128), jnp.float32)
            return c

        lax.fori_loop(0, levels, body, 0, unroll=2)

    cosine = register_order(cos_ref[...])
    ground = register_order(ground_ref[...])
    dir_rate = -LOG2E / cosine
    dif_rate = -LOG2E * DIFFUSIVITY
    g0 = chunk * G_CHUNK
    oz = [oz_s[g0 + j] for j in range(G_CHUNK)]
    ext = [ext_s[g0 + j] for j in range(G_CHUNK)]
    half_alb = [0.5 * alb_s[g0 + j] for j in range(G_CHUNK)]

    def upward(i, carry):
        l = levels - 1 - i
        alb_dif, alb_dir = carry
        vapour, cloud, ozone = coarse[0, l], coarse[1, l], coarse[2, l]
        new_dif, new_dir = [], []
        for j in range(G_CHUNK):
            cloud_depth = cloud * ext[j]
            depth = (vapour * vap_s[l, g0 + j] + ozone * oz[j]) + cloud_depth
            half_w = (cloud_depth * half_alb[j]) / depth
            t_dir = jnp.exp2(depth * dir_rate)
            t_dif = jnp.exp2(depth * dif_rate)
            t_sq = t_dif * t_dif
            r_dif = half_w * (1.0 - t_sq)
            s_dir = half_w * (1.0 - t_dir)
            den = 1.0 / (1.0 - r_dif * alb_dif[j])
            through = alb_dir[j] * t_dir
            down = (s_dir + r_dif * through) * den
            k_tdir[l, j] = t_dir
            k_a[l, j] = t_dif * den
            k_b[l, j] = down
            k_ad[l, j] = alb_dif[j]
            k_as[l, j] = alb_dir[j]
            new_dir.append(s_dir + t_dif * (alb_dif[j] * down + through))
            new_dif.append(r_dif + t_sq * alb_dif[j] * den)
        return tuple(new_dif), tuple(new_dir)

    start = (ground,) * G_CHUNK
    _, top_dir = lax.fori_loop(0, levels, upward, (start, start))

    direct0 = tuple(cosine * sol_s[g0 + j] for j in range(G_CHUNK))
    net0 = tuple(d - t * d for d, t in zip(direct0, top_dir))
    diffuse0 = tuple(jnp.zeros((8, 128), jnp.float32) for _ in range(G_CHUNK))

    def downward(l, carry):
        direct, diffuse, net = carry
        n_direct, n_diffuse, n_net = [], [], []
        sums = None
        for j in range(G_CHUNK):
            s_low = direct[j] * k_tdir[l, j]
            d_low = diffuse[j] * k_a[l, j] + direct[j] * k_b[l, j]
            up = k_ad[l, j] * d_low + k_as[l, j] * s_low
            total = s_low + d_low
            low_net = total - up
            terms = (net[j] - low_net, total, up, s_low)
            sums = terms if sums is None else tuple(a + b for a, b in zip(sums, terms))
            n_direct.append(s_low)
            n_diffuse.append(d_low)
            n_net.append(low_net)
        for f in range(4):
            acc[f, l] += sums[f]
        return tuple(n_direct), tuple(n_diffuse), tuple(n_net)

    lax.fori_loop(0, levels, downward, (direct0, diffuse0, net0))

    @pl.when(chunk == pl.num_programs(0) - 1)
    def _():
        lit = register_order(lit_ref[...]).astype(jnp.float32)

        def body(l, c):
            scale = jnp.full((8, 128), float(levels)) / jnp.full((8, 128), mass_s[l])
            for f in range(4):
                value = acc[f, l] * lit
                if f == 0:
                    value = value * scale
                    heat_ref[l] = value
                for xh in range(2):
                    for yh in range(2):
                        out_ref[f, l, 8 * xh : 8 * xh + 8, 128 * yh : 128 * yh + 128] = (
                            spread_part(value, xh, yh)
                        )
            return c

        lax.fori_loop(0, levels, body, 0)


def radiation(prognostic, daylit, cos_zenith, albedo, optics):
    fields, levels, cells_x, cells_y = prognostic.shape
    g_points = optics[1].shape[1]
    smem = pl.BlockSpec(memory_space=pltpu.SMEM)
    vec = pl.BlockSpec((8, 128), lambda c: (0, 0))
    whole = pl.BlockSpec(prognostic.shape, lambda c: (0, 0, 0, 0), pipeline_mode=pl.Buffered(1))
    kept = pltpu.VMEM((levels, G_CHUNK, 8, 128), jnp.float32)
    return pl.pallas_call(
        radiation_kernel,
        grid=(g_points // G_CHUNK,),
        in_specs=[smem] * 6 + [vec] * 3 + [whole],
        out_specs=[
            pl.BlockSpec(prognostic.shape, lambda c: (0, 0, 0, 0)),
            pl.BlockSpec((levels, 8, 128), lambda c: (0, 0, 0)),
        ],
        out_shape=[
            jax.ShapeDtypeStruct(prognostic.shape, jnp.float32),
            jax.ShapeDtypeStruct((levels, 8, 128), jnp.float32),
        ],
        scratch_shapes=[
            pltpu.VMEM((3, levels, 8, 128), jnp.float32),
            pltpu.VMEM((4, levels, 8, 128), jnp.float32),
            kept, kept, kept, kept, kept,
        ],
        compiler_params=pltpu.CompilerParams(vmem_limit_bytes=VMEM_LIMIT),
        name="radiation",
    )(
        *optics,
        daylit.reshape(8, 128), cos_zenith.reshape(8, 128), albedo.reshape(8, 128),
        prognostic,
    )


def dynamics_kernel(
    prog_ref, cour_ref, left_ref, right_ref, out_ref, first, row_m1, row_15, row_16, flux_16
):
    fields, block, cells_x, cells_y = prog_ref.shape
    shape = (cells_x, cells_y)
    row = lax.broadcasted_iota(jnp.int32, shape, 0)
    wall = (lax.broadcasted_iota(jnp.int32, shape, 1) > 0).astype(jnp.float32)
    is_first, is_last = row == 0, row == cells_x - 1
    last = cells_x - 1

    def before_x(value, halo):
        return jnp.where(is_first, halo, pltpu.roll(value, 1, 0))

    def after_x(value, halo):
        return jnp.where(is_last, halo, pltpu.roll(value, cells_x - 1, 0))

    def spread_y(flux):
        return pltpu.roll(flux, cells_y - 1, 1) - flux

    def pass_one(l, c):
        u = cour_ref[0, l]
        v = cour_ref[1, l] * wall
        up, um = jnp.maximum(u, 0.0), jnp.minimum(u, 0.0)
        vp, vm = jnp.maximum(v, 0.0), jnp.minimum(v, 0.0)
        u16 = right_ref[2 * fields, pl.ds(l, 1), :]
        up16, um16 = jnp.maximum(u16, 0.0), jnp.minimum(u16, 0.0)
        for f in range(fields):
            p = prog_ref[f, l]
            flux = up * before_x(p, left_ref[f, pl.ds(l, 1), :]) + um * p
            end = up16 * p[last:] + um16 * right_ref[f, pl.ds(l, 1), :]
            flux_y = vp * pltpu.roll(p, 1, 1) + vm * p
            result = p - (after_x(flux, end) - flux) - spread_y(flux_y)
            first[f, l] = result
            row_15[f, pl.ds(l, 1), :] = result[last:]
            row_m1[f, pl.ds(l, 1), :] = left_ref[fields + f, pl.ds(l, 1), :] - flux[:1]
            row_16[f, pl.ds(l, 1), :] = right_ref[fields + f, pl.ds(l, 1), :] + end
        return c

    lax.fori_loop(0, block, pass_one, 0)

    u16 = right_ref[2 * fields]
    gain16 = jnp.abs(u16) - u16 * u16
    for f in range(fields):
        lo, hi = row_15[f], row_16[f]
        speed = gain16 * (hi - lo) / (hi + lo)
        flux_16[f] = jnp.maximum(speed, 0.0) * lo + jnp.minimum(speed, 0.0) * hi

    def pass_two(l, c):
        u = cour_ref[0, l]
        v = cour_ref[1, l] * wall
        gain_x = jnp.abs(u) - u * u
        gain_y = jnp.abs(v) - v * v
        for f in range(fields):
            p = first[f, l]
            lo = before_x(p, row_m1[f, pl.ds(l, 1), :])
            speed = gain_x * (p - lo) / (p + lo)
            flux = jnp.maximum(speed, 0.0) * lo + jnp.minimum(speed, 0.0) * p
            lo = pltpu.roll(p, 1, 1)
            speed = gain_y * (p - lo) / (p + lo)
            flux_y = jnp.maximum(speed, 0.0) * lo + jnp.minimum(speed, 0.0) * p
            end = flux_16[f, pl.ds(l, 1), :]
            out_ref[f, l] = p - (after_x(flux, end) - flux) - spread_y(flux_y)
        return c

    lax.fori_loop(0, block, pass_two, 0)


def advance(prognostic, courant, left, right):
    fields, levels, cells_x, cells_y = prognostic.shape
    block = LEVEL_BLOCK
    rows = pltpu.VMEM((fields, block, cells_y), jnp.float32)
    return pl.pallas_call(
        dynamics_kernel,
        grid=(levels // block,),
        in_specs=[
            pl.BlockSpec((fields, block, cells_x, cells_y), lambda i: (0, i, 0, 0)),
            pl.BlockSpec((2, block, cells_x, cells_y), lambda i: (0, i, 0, 0)),
            pl.BlockSpec((left.shape[0], block, cells_y), lambda i: (0, i, 0)),
            pl.BlockSpec((right.shape[0], block, cells_y), lambda i: (0, i, 0)),
        ],
        out_specs=pl.BlockSpec((fields, block, cells_x, cells_y), lambda i: (0, i, 0, 0)),
        out_shape=jax.ShapeDtypeStruct(prognostic.shape, jnp.float32),
        scratch_shapes=[
            pltpu.VMEM((fields, block, cells_x, cells_y), jnp.float32), rows, rows, rows, rows,
        ],
        compiler_params=pltpu.CompilerParams(vmem_limit_bytes=VMEM_LIMIT),
        name="advance",
    )(prognostic, courant, left, right)


def warm_kernel(field_ref, heat_ref, out_ref):
    def body(l, c):
        packed = heat_ref[l] * STEP_LENGTH
        for xh in range(2):
            for yh in range(2):
                part = (0, l, slice(8 * xh, 8 * xh + 8), slice(128 * yh, 128 * yh + 128))
                out_ref[part] = field_ref[part] + spread_part(packed, xh, yh)
        return c

    lax.fori_loop(0, heat_ref.shape[0], body, 0, unroll=4)


def warm(fields, heat):
    _, levels, cells_x, cells_y = fields.shape
    block = 16
    spec = pl.BlockSpec((1, block, cells_x, cells_y), lambda i: (0, i, 0, 0))
    return pl.pallas_call(
        warm_kernel,
        grid=(levels // block,),
        in_specs=[spec, pl.BlockSpec((block, 8, 128), lambda i: (i, 0, 0))],
        out_specs=spec,
        out_shape=jax.ShapeDtypeStruct(fields.shape, jnp.float32),
        input_output_aliases={0: 0},
        name="warm",
    )(fields, heat)


def upwind(low, high, face):
    return jnp.maximum(face, 0.0) * low + jnp.minimum(face, 0.0) * high


def across_y(value, face):
    flux = upwind(jnp.roll(value, 1, axis=-1), value, face)
    return jnp.roll(flux, -1, axis=-1) - flux


def edge_rows(prognostic, courant):
    u, v = courant
    wall = (lax.iota(jnp.int32, v.shape[-1]) > 0).astype(jnp.float32)
    end, inner = prognostic[:, :, -1], prognostic[:, :, -2]
    partial = end + upwind(inner, end, u[:, -1]) - across_y(end, v[:, -1] * wall)
    to_right = jnp.concatenate([end, partial], axis=0)
    start, inner = prognostic[:, :, 0], prognostic[:, :, 1]
    partial = start - upwind(start, inner, u[:, 1]) - across_y(start, v[:, 0] * wall)
    to_left = jnp.concatenate([start, partial, u[None, :, 0]], axis=0)
    return to_right, to_left


def per_device(prognostic, courant, daylit, cos_zenith, albedo, *optics):
    dynamics = lax.axis_index("grp") == 0
    tiles = lax.axis_size("tile")
    to_right, to_left = edge_rows(prognostic, courant)
    left = lax.ppermute(to_right, ("grp", "tile"), [(i, (i + 1) % tiles) for i in range(tiles)])
    right = lax.ppermute(to_left, ("grp", "tile"), [((i + 1) % tiles, i) for i in range(tiles)])
    levels = prognostic.shape[1]

    def run_dynamics(left, right):
        return advance(prognostic, courant, left, right), jnp.zeros((levels, 8, 128), jnp.float32)

    def run_radiation(left, right):
        out, heat = radiation(prognostic, daylit, cos_zenith, albedo, optics)
        return out, heat

    fields, heat = lax.cond(dynamics, run_dynamics, run_radiation, left, right)
    heat = lax.ppermute(heat, "grp", [(1, 0)])
    return warm(fields, heat)[None]


def solution(mesh):
    column = P("tile")
    plane = P(None, None, "tile", None)
    return jax.shard_map(
        per_device,
        mesh=mesh,
        in_specs=(plane, plane, column, column, column) + (P(),) * 6,
        out_specs=P("grp", None, None, "tile", None),
        check_vma=False,
    )
```

profile of v0, /device:TPU:0, one launch (start us, length us, event | category | flops | bytes accessed | tf_op | source)
XLA Modules:
  0.0 64.7 jit_solution(8634129772800662049)
XLA Ops:
  0.0 0.0 copy-start
  0.0 4.6 %fusion.15 = (f32[4,64,1,256]{3,2,1,0:T(1,128)S(1)}, f32[4,64,1,256]{3,2,1,0:T(1,128)S(1)}, f32[4,64,1,256]{3,2,1,0:T(1,128)S(1)}, f32[4,64,1,256]{3,2,1,0:T(1,128)S(1)}) fusion(f32[4,64,16,256]{3,2,1,0:T(8,128)} %param.13), kind=kLoop, calls=%fused_computation.35 | loop fusion | bytes 2097152 | tf_op jit(solution)/shard_map/slice | solution.py:315
  4.6 0.1 slice.80
  4.8 0.1 slice.74
  4.9 0.0 copy-done
  4.9 0.2 fusion.16
  5.1 0.1 fusion.17
  5.2 0.2 fusion
  5.4 0.1 slice.82
  5.6 0.0 copy-start.2
  5.6 0.0 copy-start.3
  5.6 0.0 copy-start.4
  5.6 0.0 copy-start.5
  5.6 0.0 copy-start.6
  5.6 0.0 copy-start.7
  5.6 0.0 copy-start.8
  5.7 0.0 copy-start.9
  5.7 0.0 copy-start.10
  5.7 0.6 copy.77
  6.3 0.1 fusion.3
  6.5 7.4 %collective-permute-start.1 = (f32[9,64,256]{2,1,0:T(8,128)S(1)}, f32[9,64,256]{2,1,0:T(8,128)S(1)}, u32[]{:S(2)}, u32[]{:S(2)}) collective-permute-start(f32[9,64,256]{2,1,0:T(8,128)S(1)} %pad_maximum_fusion), channel_id=1, source_target_pairs={{1,0},{2,1},{3,2},{4,3},{5,4},{6,5},{7,6},{8,7},{9,8},{10,9},{11,1... | collective-permute-start | bytes 1769480 | tf_op jit(solution)/shard_map/ppermute | solution.py:326
  13.9 0.1 slice.76
  14.0 0.1 fusion.1
  14.2 0.8 %pad_maximum_fusion.1 = f32[8,64,256]{2,1,0:T(8,128)} fusion(f32[4,64,256]{2,1,0:T(8,128)S(1)} %fusion.1, f32[4,64,256]{2,1,0:T(8,128)S(1)} %bitcast.71), kind=kLoop, calls=%fused_computation.3 | loop fusion | flops 131072 | bytes 1048576 | tf_op jit(solution)/shard_map/concatenate | solution.py:314
  15.0 1.9 %collective-permute-start = (f32[8,64,256]{2,1,0:T(8,128)}, f32[8,64,256]{2,1,0:T(8,128)}, u32[]{:S(2)}, u32[]{:S(2)}) collective-permute-start(f32[8,64,256]{2,1,0:T(8,128)} %pad_maximum_fusion.1), channel_id=1, source_target_pairs={{0,1},{1,2},{2,3},{3,4},{4,5},{5,6},{6,7},{7,8},{8,9},{9,10},{10,1... | collective-permute-start | bytes 1572872 | tf_op jit(solution)/shard_map/ppermute | solution.py:325
  16.9 11.6 %collective-permute-done = f32[8,64,256]{2,1,0:T(8,128)} collective-permute-done((f32[8,64,256]{2,1,0:T(8,128)}, f32[8,64,256]{2,1,0:T(8,128)}, u32[]{:S(2)}, u32[]{:S(2)}) %collective-permute-start) | collective-permute-done | bytes 524320 | tf_op jit(solution)/shard_map/ppermute | solution.py:325
  28.5 0.0 collective-permute-done.1
  28.5 0.0 copy-done.2
  28.5 0.0 copy-done.3
  28.5 0.0 copy-done.4
  28.5 0.0 copy-done.5
  28.6 0.0 copy-done.6
  28.6 0.0 copy-done.7
  28.6 0.0 copy-done.8
  28.6 0.0 copy-done.9
  28.6 0.0 copy-done.10
  28.6 23.7 %conditional.1 = ((f32[4,64,16,256]{3,2,1,0:T(8,128)}, f32[64,8,128]{2,1,0:T(8,128)S(1)})) conditional(s32[]{:T(128)} %convert_element_type.12, (s32[1024]{0:T(1024)S(1)}, f32[1024]{0:T(1024)S(1)}, f32[1024]{0:T(1024)S(1)}, f32[64]{0:T(128)S(1)}, f32[64,32]{0,1:T(8,128)S(1)}, /*index=5*/f32[32]{0:T(128)S(1)}, f32[32]{0:T(128)S(1)}, f32[32]{0:T(128)S(1)}, ...), branch_computations={%region_0.1_spmd, %region_1.2_spmd} | conditional | bytes 262172 | solution.py:336
  28.6 23.6 %advance.1 = f32[4,64,16,256]{3,2,1,0:T(8,128)} custom-call(f32[4,64,16,256]{3,2,1,0:T(8,128)} %get-tuple-element.43.prog_ref, f32[2,64,16,256]{3,2,1,0:T(8,128)S(1)} %get-tuple-element.44.cour_ref, f32[8,64,256]{2,1,0:T(8,128)} %get-tuple-element.45.left_ref, f32[9,64,256]{2,1,0:T(8,128)S(1)} %get-tuple-element.46.right_ref), custom_call_target="tpu_custom_call" | custom-call | tf_op jit(solution)/shard_map/cond/branch_1_fun/advance/pallas_call | solution.py:254
  52.3 1.3 %collective-permute-start.2 = (f32[64,8,128]{2,1,0:T(8,128)S(1)}, f32[64,8,128]{2,1,0:T(8,128)S(1)}, u32[]{:S(2)}, u32[]{:S(2)}) collective-permute-start(f32[64,8,128]{2,1,0:T(8,128)S(1)} %get-tuple-element.50), channel_id=1, source_target_pairs={{16,0},{17,1},{18,2},{19,3},{20,4},{21,5},{22,6},{23,7},{24,8},{25... | collective-permute-start | bytes 786440 | tf_op jit(solution)/shard_map/ppermute | solution.py:337
  53.6 7.0 %collective-permute-done.2.heat_ref = f32[64,8,128]{2,1,0:T(8,128)S(1)} collective-permute-done((f32[64,8,128]{2,1,0:T(8,128)S(1)}, f32[64,8,128]{2,1,0:T(8,128)S(1)}, u32[]{:S(2)}, u32[]{:S(2)}) %collective-permute-start.2) | collective-permute-done | bytes 262176 | tf_op jit(solution)/shard_map/ppermute | solution.py:337
  60.5 0.0 copy-start.1
  60.5 0.7 %copy-done.1 = f32[64,8,128]{2,1,0:T(8,128)} copy-done((f32[64,8,128]{2,1,0:T(8,128)}, f32[64,8,128]{2,1,0:T(8,128)S(1)}, u32[]{:S(2)}) %copy-start.1) | copy-done | bytes 262168
  61.2 3.4 %warm.1 = f32[4,64,16,256]{3,2,1,0:T(8,128)} custom-call(f32[4,64,16,256]{3,2,1,0:T(8,128)} %get-tuple-element.49.field_ref, f32[64,8,128]{2,1,0:T(8,128)} %copy-done.1), custom_call_target="tpu_custom_call", output_to_operand_aliasing={{}: (0, {})} | custom-call | tf_op jit(solution)/shard_map/warm/pallas_call | solution.py:289
  (9 shorter events, 0.2 us)
Async XLA Ops:
  0.0 4.9 %copy-start = (f32[2,64,16,256]{3,2,1,0:T(8,128)S(1)}, f32[2,64,16,256]{3,2,1,0:T(8,128)}, u32[]{:S(2)}) copy-start(f32[2,64,16,256]{3,2,1,0:T(8,128)} %param.14) | copy-start | bytes 6291460
  5.6 23.0 %copy-start.2 = (f32[64,32]{0,1:T(8,128)S(1)}, f32[64,32]{0,1:T(8,128)}, u32[]{:S(2)}) copy-start(f32[64,32]{0,1:T(8,128)} %param.19) | copy-start | bytes 24580
  5.6 22.9 %copy-start.3 = (s32[1024]{0:T(1024)S(1)}, s32[1024]{0:T(1024)}, u32[]{:S(2)}) copy-start(s32[1024]{0:T(1024)} %param.15) | copy-start | bytes 12292
  5.6 22.9 %copy-start.4 = (f32[1024]{0:T(1024)S(1)}, f32[1024]{0:T(1024)}, u32[]{:S(2)}) copy-start(f32[1024]{0:T(1024)} %param.16) | copy-start | bytes 12292
  5.6 22.9 %copy-start.5 = (f32[1024]{0:T(1024)S(1)}, f32[1024]{0:T(1024)}, u32[]{:S(2)}) copy-start(f32[1024]{0:T(1024)} %param.17) | copy-start | bytes 12292
  5.6 22.9 %copy-start.6 = (f32[64]{0:T(128)S(1)}, f32[64]{0:T(128)}, u32[]{:S(2)}) copy-start(f32[64]{0:T(128)} %param.18) | copy-start | bytes 772
  5.6 22.9 %copy-start.7 = (f32[32]{0:T(128)S(1)}, f32[32]{0:T(128)}, u32[]{:S(2)}) copy-start(f32[32]{0:T(128)} %param.20) | copy-start | bytes 388
  5.6 22.9 %copy-start.8 = (f32[32]{0:T(128)S(1)}, f32[32]{0:T(128)}, u32[]{:S(2)}) copy-start(f32[32]{0:T(128)} %param.21) | copy-start | bytes 388
  5.7 22.9 %copy-start.9 = (f32[32]{0:T(128)S(1)}, f32[32]{0:T(128)}, u32[]{:S(2)}) copy-start(f32[32]{0:T(128)} %param.22) | copy-start | bytes 388
  5.7 22.9 %copy-start.10 = (f32[32]{0:T(128)S(1)}, f32[32]{0:T(128)}, u32[]{:S(2)}) copy-start(f32[32]{0:T(128)} %param.23) | copy-start | bytes 388
  6.5 22.0 %collective-permute-start.1 = (f32[9,64,256]{2,1,0:T(8,128)S(1)}, f32[9,64,256]{2,1,0:T(8,128)S(1)}, u32[]{:S(2)}, u32[]{:S(2)}) collective-permute-start(f32[9,64,256]{2,1,0:T(8,128)S(1)} %pad_maximum_fusion), channel_id=1, source_target_pairs={{1,0},{2,1},{3,2},{4,3},{5,4},{6,5},{7,6},{8,7},{9,8},{10,9},{11,1... | collective-permute-start | bytes 1769480 | tf_op jit(solution)/shard_map/ppermute | solution.py:326
  15.0 13.5 %collective-permute-start = (f32[8,64,256]{2,1,0:T(8,128)}, f32[8,64,256]{2,1,0:T(8,128)}, u32[]{:S(2)}, u32[]{:S(2)}) collective-permute-start(f32[8,64,256]{2,1,0:T(8,128)} %pad_maximum_fusion.1), channel_id=1, source_target_pairs={{0,1},{1,2},{2,3},{3,4},{4,5},{5,6},{6,7},{7,8},{8,9},{9,10},{10,1... | collective-permute-start | bytes 1572872 | tf_op jit(solution)/shard_map/ppermute | solution.py:325
  52.3 8.3 %collective-permute-start.2 = (f32[64,8,128]{2,1,0:T(8,128)S(1)}, f32[64,8,128]{2,1,0:T(8,128)S(1)}, u32[]{:S(2)}, u32[]{:S(2)}) collective-permute-start(f32[64,8,128]{2,1,0:T(8,128)S(1)} %get-tuple-element.50), channel_id=1, source_target_pairs={{16,0},{17,1},{18,2},{19,3},{20,4},{21,5},{22,6},{23,7},{24,8},{25... | collective-permute-start | bytes 786440 | tf_op jit(solution)/shard_map/ppermute | solution.py:337
  60.5 0.7 %copy-start.1 = (f32[64,8,128]{2,1,0:T(8,128)}, f32[64,8,128]{2,1,0:T(8,128)S(1)}, u32[]{:S(2)}) copy-start(f32[64,8,128]{2,1,0:T(8,128)S(1)} %collective-permute-done.2.heat_ref) | copy-start | bytes 786436
where the time goes:
time: 64.9 us; the launch traced here: 64.7 us
  Pallas kernels  27.1 us (42%)
  waiting for transfers between devices  18.5 us (29%)
  starting transfers between devices  10.6 us (16%)
  local copies, waits for them, and re-layouts  6.74 us (10%)
  other arithmetic  1.44 us (2%)
    pallas_call x1, Pallas kernels, advance(): pl.pallas_call(dynamics_kernel, grid=(levels // block,), in_specs=[pl.Blo...  23.6 us
    ppermute x1, waiting for transfers between devices, per_device(): lax.ppermute(to_right, ('grp', 'tile'), [(i, (i + 1) % tiles) for i in ra...  11.6 us
    ppermute x1, starting transfers between devices, per_device(): lax.ppermute(to_left, ('grp', 'tile'), [((i + 1) % tiles, i) for i in ran...  7.35 us
    ppermute x1, waiting for transfers between devices, per_device(): heat = lax.ppermute(heat, 'grp', [(1, 0)])  6.97 us
    slice x1, local copies, waits for them, and re-layouts, edge_rows(): start, inner = (prognostic[:, :, 0], prognostic[:, :, 1])  4.6 us
    pallas_call x1, Pallas kernels, warm(): pl.pallas_call(warm_kernel, grid=(levels // block,), in_specs=[spec, pl.B...  3.43 us
    ppermute x1, starting transfers between devices, per_device(): lax.ppermute(to_right, ('grp', 'tile'), [(i, (i + 1) % tiles) for i in ra...  1.91 us
    unnamed x25, local copies, waits for them, and re-layouts  1.41 us
  transfers between devices with their start and end apart: 3, of which 2 were waited for; matrix products, arithmetic and copies ran while one was open for 2% of the time, Pallas kernels for 0%

commit v1 on v0

v1 whole, which is shorter than its diff:
```python
import functools

import jax
import jax.numpy as jnp
from jax import lax
from jax.experimental import pallas as pl
from jax.experimental.pallas import tpu as pltpu
from jax.sharding import PartitionSpec as P

COARSEN = 4
DIFFUSIVITY = 1.66
STEP_LENGTH = 1.0
LOG2E = 1.4426950408889634
G_CHUNK = 8
LEVEL_BLOCK = 8
VMEM_LIMIT = 56 * 1024 * 1024


def pack_means(tile):
    sub = lax.broadcasted_iota(jnp.int32, (8, 128), 0) % 4
    packed = None
    for xh in range(2):
        for yh in range(2):
            part = tile[8 * xh : 8 * xh + 8, 128 * yh : 128 * yh + 128]
            part = part + pltpu.roll(part, 7, 0)
            part = part + pltpu.roll(part, 6, 0)
            k = 2 * xh + yh
            if k:
                part = pltpu.roll(part, k, 0)
            packed = part if packed is None else jnp.where(sub == k, part, packed)
    return packed * (1.0 / COARSEN)


def spread_part(packed, xh, yh):
    k = 2 * xh + yh
    low = jnp.broadcast_to(packed[k : k + 1], (8, 128))
    high = jnp.broadcast_to(packed[4 + k : 5 + k], (8, 128))
    return jnp.where(lax.broadcasted_iota(jnp.int32, (8, 128), 0) < 4, low, high)


def register_order(rows):
    return jnp.concatenate([rows[0:2], rows[4:6], rows[2:4], rows[6:8]], axis=0)


def radiation_kernel(
    mass_s, vap_s, oz_s, ext_s, alb_s, sol_s,
    lit_ref, cos_ref, ground_ref, vapour_ref, cloud_ref, ozone_ref,
    unused_ref, heat_ref, acc,
    coarse, k_tdir, k_a, k_b, k_ad, k_as,
):
    chunk = pl.program_id(0)
    levels = acc.shape[1]

    @pl.when(chunk == 0)
    def _():
        def body(l, c):
            scale = mass_s[l]
            for f, ref in enumerate((vapour_ref, cloud_ref, ozone_ref)):
                coarse[f, l] = pack_means(ref[0, l]) * scale
            for f in range(4):
                acc[f, l] = jnp.zeros((8, 128), jnp.float32)
            return c

        lax.fori_loop(0, levels, body, 0, unroll=2)

    cosine = register_order(cos_ref[...])
    ground = register_order(ground_ref[...])
    dir_rate = -LOG2E / cosine
    dif_rate = -LOG2E * DIFFUSIVITY
    g0 = chunk * G_CHUNK
    oz = [oz_s[g0 + j] for j in range(G_CHUNK)]
    ext = [ext_s[g0 + j] for j in range(G_CHUNK)]
    half_alb = [0.5 * alb_s[g0 + j] for j in range(G_CHUNK)]

    def upward(i, carry):
        l = levels - 1 - i
        alb_dif, alb_dir = carry
        vapour, cloud, ozone = coarse[0, l], coarse[1, l], coarse[2, l]
        new_dif, new_dir = [], []
        for j in range(G_CHUNK):
            cloud_depth = cloud * ext[j]
            depth = (vapour * vap_s[l, g0 + j] + ozone * oz[j]) + cloud_depth
            half_w = (cloud_depth * half_alb[j]) * inverse(depth)
            t_dir = jnp.exp2(depth * dir_rate)
            t_dif = jnp.exp2(depth * dif_rate)
            t_sq = t_dif * t_dif
            r_dif = half_w * (1.0 - t_sq)
            s_dir = half_w * (1.0 - t_dir)
            den = inverse(1.0 - r_dif * alb_dif[j])
            through = alb_dir[j] * t_dir
            down = (s_dir + r_dif * through) * den
            k_tdir[l, j] = t_dir
            k_a[l, j] = t_dif * den
            k_b[l, j] = down
            k_ad[l, j] = alb_dif[j]
            k_as[l, j] = alb_dir[j]
            new_dir.append(s_dir + t_dif * (alb_dif[j] * down + through))
            new_dif.append(r_dif + t_sq * alb_dif[j] * den)
        return tuple(new_dif), tuple(new_dir)

    start = (ground,) * G_CHUNK
    _, top_dir = lax.fori_loop(0, levels, upward, (start, start))

    direct0 = tuple(cosine * sol_s[g0 + j] for j in range(G_CHUNK))
    net0 = tuple(d - t * d for d, t in zip(direct0, top_dir))
    diffuse0 = tuple(jnp.zeros((8, 128), jnp.float32) for _ in range(G_CHUNK))

    def downward(l, carry):
        direct, diffuse, net = carry
        n_direct, n_diffuse, n_net = [], [], []
        sums = None
        for j in range(G_CHUNK):
            s_low = direct[j] * k_tdir[l, j]
            d_low = diffuse[j] * k_a[l, j] + direct[j] * k_b[l, j]
            up = k_ad[l, j] * d_low + k_as[l, j] * s_low
            total = s_low + d_low
            low_net = total - up
            terms = (net[j] - low_net, total, up, s_low)
            sums = terms if sums is None else tuple(a + b for a, b in zip(sums, terms))
            n_direct.append(s_low)
            n_diffuse.append(d_low)
            n_net.append(low_net)
        for f in range(4):
            acc[f, l] += sums[f]
        return tuple(n_direct), tuple(n_diffuse), tuple(n_net)

    lax.fori_loop(0, levels, downward, (direct0, diffuse0, net0))

    @pl.when(chunk == pl.num_programs(0) - 1)
    def _():
        lit = register_order(lit_ref[...]).astype(jnp.float32)

        def body(l, c):
            heat_ref[l] = acc[0, l] * lit * (float(levels) / jnp.full((8, 128), mass_s[l]))
            return c

        lax.fori_loop(0, levels, body, 0, unroll=4)


def radiation(prognostic, daylit, cos_zenith, albedo, optics):
    fields, levels, cells_x, cells_y = prognostic.shape
    g_points = optics[1].shape[1]
    smem = pl.BlockSpec(memory_space=pltpu.SMEM)
    vec = pl.BlockSpec((8, 128), lambda c: (0, 0))
    field_specs = [
        pl.BlockSpec(
            (1, levels, cells_x, cells_y), lambda c, f=f: (f, 0, 0, 0), pipeline_mode=pl.Buffered(1)
        )
        for f in range(1, 4)
    ]
    kept = pltpu.VMEM((levels, G_CHUNK, 8, 128), jnp.float32)
    return pl.pallas_call(
        radiation_kernel,
        grid=(g_points // G_CHUNK,),
        in_specs=[smem] * 6 + [vec] * 3 + field_specs,
        out_specs=[
            pl.BlockSpec(memory_space=pl.ANY),
            pl.BlockSpec((levels, 8, 128), lambda c: (0, 0, 0)),
            pl.BlockSpec((4, levels, 8, 128), lambda c: (0, 0, 0, 0)),
        ],
        out_shape=[
            jax.ShapeDtypeStruct(prognostic.shape, jnp.float32),
            jax.ShapeDtypeStruct((levels, 8, 128), jnp.float32),
            jax.ShapeDtypeStruct((4, levels, 8, 128), jnp.float32),
        ],
        scratch_shapes=[pltpu.VMEM((3, levels, 8, 128), jnp.float32), kept, kept, kept, kept, kept],
        compiler_params=pltpu.CompilerParams(vmem_limit_bytes=VMEM_LIMIT),
        name="radiation",
    )(
        *optics,
        daylit.reshape(8, 128), cos_zenith.reshape(8, 128), albedo.reshape(8, 128),
        prognostic, prognostic, prognostic,
    )


def expand_kernel(lit_ref, heat_ref, acc_ref, out_ref):
    lit = register_order(lit_ref[...]).astype(jnp.float32)

    def body(l, c):
        for f in range(4):
            value = heat_ref[l] if f == 0 else acc_ref[f, l] * lit
            for xh in range(2):
                for yh in range(2):
                    out_ref[f, l, 8 * xh : 8 * xh + 8, 128 * yh : 128 * yh + 128] = spread_part(
                        value, xh, yh
                    )
        return c

    lax.fori_loop(0, heat_ref.shape[0], body, 0, unroll=2)


def expand(daylit, heat, fluxes, shape):
    fields, levels, cells_x, cells_y = shape
    block = LEVEL_BLOCK
    return pl.pallas_call(
        expand_kernel,
        grid=(levels // block,),
        in_specs=[
            pl.BlockSpec((8, 128), lambda i: (0, 0)),
            pl.BlockSpec((block, 8, 128), lambda i: (i, 0, 0)),
            pl.BlockSpec((4, block, 8, 128), lambda i: (0, i, 0, 0)),
        ],
        out_specs=pl.BlockSpec((fields, block, cells_x, cells_y), lambda i: (0, i, 0, 0)),
        out_shape=jax.ShapeDtypeStruct(shape, jnp.float32),
        name="expand",
    )(daylit.reshape(8, 128), heat, fluxes)


def inverse(value):
    return pl.reciprocal(value, approx=False)


def wall_mask(shape):
    return (lax.broadcasted_iota(jnp.int32, shape, len(shape) - 1) > 0).astype(jnp.float32)


def upwind(low, high, face):
    return jnp.maximum(face, 0.0) * low + jnp.minimum(face, 0.0) * high


def across_y(value, face):
    flux = upwind(pltpu.roll(value, 1, 1), value, face)
    return pltpu.roll(flux, value.shape[1] - 1, 1) - flux


def edges_kernel(prog_ref, cour_ref, right_ref, left_ref, rows):
    fields, block, cells_x, cells_y = prog_ref.shape
    last = cells_x - 1
    picks = [(prog_ref, f, x) for x in (last, last - 1, 0, 1) for f in range(fields)]
    picks += [(cour_ref, 0, last), (cour_ref, 0, 1), (cour_ref, 0, 0), (cour_ref, 1, last), (cour_ref, 1, 0)]
    for l in range(block):
        for k, (ref, f, x) in enumerate(picks):
            rows[k, l : l + 1, :] = ref[f, l, x : x + 1, :]
    base = 4 * fields
    u_last, u_one, u_zero = rows[base], rows[base + 1], rows[base + 2]
    wall = wall_mask((block, cells_y))
    v_last, v_zero = rows[base + 3] * wall, rows[base + 4] * wall
    for f in range(fields):
        end, inner = rows[f], rows[fields + f]
        right_ref[f] = end
        right_ref[fields + f] = end + upwind(inner, end, u_last) - across_y(end, v_last)
        start, inner = rows[2 * fields + f], rows[3 * fields + f]
        left_ref[f] = start
        left_ref[fields + f] = start - upwind(start, inner, u_one) - across_y(start, v_zero)
    left_ref[2 * fields] = u_zero


def edges(prognostic, courant):
    fields, levels, cells_x, cells_y = prognostic.shape
    block = LEVEL_BLOCK
    return pl.pallas_call(
        edges_kernel,
        grid=(levels // block,),
        in_specs=[
            pl.BlockSpec((fields, block, cells_x, cells_y), lambda i: (0, i, 0, 0)),
            pl.BlockSpec((2, block, cells_x, cells_y), lambda i: (0, i, 0, 0)),
        ],
        out_specs=[
            pl.BlockSpec((2 * fields, block, cells_y), lambda i: (0, i, 0)),
            pl.BlockSpec((2 * fields + 1, block, cells_y), lambda i: (0, i, 0)),
        ],
        out_shape=[
            jax.ShapeDtypeStruct((2 * fields, levels, cells_y), jnp.float32),
            jax.ShapeDtypeStruct((2 * fields + 1, levels, cells_y), jnp.float32),
        ],
        scratch_shapes=[pltpu.VMEM((4 * fields + 5, block, cells_y), jnp.float32)],
        name="edges",
    )(prognostic, courant)


def no_edges(prognostic):
    fields, levels, _, cells_y = prognostic.shape
    return pl.pallas_call(
        lambda right_ref, left_ref: None,
        out_specs=[pl.BlockSpec(memory_space=pl.ANY)] * 2,
        out_shape=[
            jax.ShapeDtypeStruct((2 * fields, levels, cells_y), jnp.float32),
            jax.ShapeDtypeStruct((2 * fields + 1, levels, cells_y), jnp.float32),
        ],
        name="no_edges",
    )()


def pass_one_kernel(prog_ref, cour_ref, first_ref, heat_ref, acc_ref):
    fields, block, cells_x, cells_y = prog_ref.shape
    shape = (cells_x, cells_y)
    wall = wall_mask(shape)
    inside = (lax.broadcasted_iota(jnp.int32, shape, 0) > 0).astype(jnp.float32)

    def body(l, c):
        u = cour_ref[0, l] * inside
        v = cour_ref[1, l] * wall
        up, um = jnp.maximum(u, 0.0), jnp.minimum(u, 0.0)
        vp, vm = jnp.maximum(v, 0.0), jnp.minimum(v, 0.0)
        for f in range(fields):
            p = prog_ref[f, l]
            flux = up * pltpu.roll(p, 1, 0) + um * p
            flux_y = vp * pltpu.roll(p, 1, 1) + vm * p
            first_ref[f, l] = (
                p
                - (pltpu.roll(flux, cells_x - 1, 0) - flux)
                - (pltpu.roll(flux_y, cells_y - 1, 1) - flux_y)
            )
        return c

    lax.fori_loop(0, block, body, 0)


def pass_one(prognostic, courant):
    fields, levels, cells_x, cells_y = prognostic.shape
    block = LEVEL_BLOCK
    plane = pl.BlockSpec((fields, block, cells_x, cells_y), lambda i: (0, i, 0, 0))
    return pl.pallas_call(
        pass_one_kernel,
        grid=(levels // block,),
        in_specs=[plane, pl.BlockSpec((2, block, cells_x, cells_y), lambda i: (0, i, 0, 0))],
        out_specs=[plane, pl.BlockSpec(memory_space=pl.ANY), pl.BlockSpec(memory_space=pl.ANY)],
        out_shape=[
            jax.ShapeDtypeStruct(prognostic.shape, jnp.float32),
            jax.ShapeDtypeStruct((levels, 8, 128), jnp.float32),
            jax.ShapeDtypeStruct((4, levels, 8, 128), jnp.float32),
        ],
        name="pass_one",
    )(prognostic, courant)


def pass_two_kernel(
    first_ref, edge_ref, cour_ref, left_ref, right_ref, out_ref, rows, row_m1, row_0, row_15, flux_16
):
    fields, block, cells_x, cells_y = first_ref.shape
    shape = (cells_x, cells_y)
    last = cells_x - 1
    row = lax.broadcasted_iota(jnp.int32, shape, 0)
    wall = wall_mask(shape)
    is_first, is_last = row == 0, row == last

    for l in range(block):
        rows[2 * fields, l : l + 1, :] = cour_ref[0, l, :1, :]
        for f in range(fields):
            rows[f, l : l + 1, :] = edge_ref[f, l, :1, :]
            rows[fields + f, l : l + 1, :] = edge_ref[f, l, last:, :]
            row_0[f, l : l + 1, :] = first_ref[f, l, :1, :]
            row_15[f, l : l + 1, :] = first_ref[f, l, last:, :]
    u0, u16 = rows[2 * fields], right_ref[2 * fields]
    gain = jnp.abs(u16) - u16 * u16
    for f in range(fields):
        begin = upwind(left_ref[f], rows[f], u0)
        end = upwind(rows[fields + f], right_ref[f], u16)
        row_m1[f] = left_ref[fields + f] - begin
        row_0[f] = row_0[f] + begin
        lo = row_15[f] - end
        hi = right_ref[fields + f] + end
        row_15[f] = lo
        speed = gain * (hi - lo) * inverse(hi + lo)
        flux_16[f] = upwind(lo, hi, speed)

    def body(l, c):
        u = cour_ref[0, l]
        v = cour_ref[1, l] * wall
        gain_x = jnp.abs(u) - u * u
        gain_y = jnp.abs(v) - v * v
        one = pl.ds(l, 1)
        for f in range(fields):
            p = first_ref[f, l]
            p = jnp.where(is_first, row_0[f, one, :], jnp.where(is_last, row_15[f, one, :], p))
            lo = jnp.where(is_first, row_m1[f, one, :], pltpu.roll(p, 1, 0))
            flux = upwind(lo, p, gain_x * (p - lo) * inverse(p + lo))
            lo = pltpu.roll(p, 1, 1)
            flux_y = upwind(lo, p, gain_y * (p - lo) * inverse(p + lo))
            beyond = jnp.where(is_last, flux_16[f, one, :], pltpu.roll(flux, last, 0))
            out_ref[f, l] = p - (beyond - flux) - (pltpu.roll(flux_y, cells_y - 1, 1) - flux_y)
        return c

    lax.fori_loop(0, block, body, 0)


def pass_two(first, prognostic, courant, left, right):
    fields, levels, cells_x, cells_y = first.shape
    block = LEVEL_BLOCK
    plane = pl.BlockSpec((fields, block, cells_x, cells_y), lambda i: (0, i, 0, 0))
    rows = pltpu.VMEM((fields, block, cells_y), jnp.float32)
    return pl.pallas_call(
        pass_two_kernel,
        grid=(levels // block,),
        in_specs=[
            plane,
            plane,
            pl.BlockSpec((2, block, cells_x, cells_y), lambda i: (0, i, 0, 0)),
            pl.BlockSpec((left.shape[0], block, cells_y), lambda i: (0, i, 0)),
            pl.BlockSpec((right.shape[0], block, cells_y), lambda i: (0, i, 0)),
        ],
        out_specs=plane,
        out_shape=jax.ShapeDtypeStruct(first.shape, jnp.float32),
        scratch_shapes=[
            pltpu.VMEM((2 * fields + 1, block, cells_y), jnp.float32), rows, rows, rows, rows,
        ],
        name="pass_two",
    )(first, prognostic, courant, left, right)


def warm_kernel(field_ref, heat_ref, out_ref):
    block = field_ref.shape[1]
    start = pl.program_id(0) * block

    def body(l, c):
        packed = heat_ref[start + l] * STEP_LENGTH
        for xh in range(2):
            for yh in range(2):
                part = (0, l, slice(8 * xh, 8 * xh + 8), slice(128 * yh, 128 * yh + 128))
                out_ref[part] = field_ref[part] + spread_part(packed, xh, yh)
        return c

    lax.fori_loop(0, block, body, 0, unroll=4)


def warm(fields, heat):
    _, levels, cells_x, cells_y = fields.shape
    block = 16
    spec = pl.BlockSpec((1, block, cells_x, cells_y), lambda i: (0, i, 0, 0))
    return pl.pallas_call(
        warm_kernel,
        grid=(levels // block,),
        in_specs=[spec, pl.BlockSpec(memory_space=pltpu.VMEM)],
        out_specs=spec,
        out_shape=jax.ShapeDtypeStruct(fields.shape, jnp.float32),
        input_output_aliases={0: 0},
        name="warm",
    )(fields, heat)


def per_device(prognostic, courant, daylit, cos_zenith, albedo, *optics):
    dynamics = lax.axis_index("grp") == 0
    tiles = lax.axis_size("tile")
    to_right, to_left = lax.cond(
        dynamics, lambda: edges(prognostic, courant), lambda: no_edges(prognostic)
    )
    left = lax.ppermute(to_right, ("grp", "tile"), [(i, (i + 1) % tiles) for i in range(tiles)])
    right = lax.ppermute(to_left, ("grp", "tile"), [((i + 1) % tiles, i) for i in range(tiles)])
    first, heat, fluxes = lax.cond(
        dynamics,
        lambda: pass_one(prognostic, courant),
        lambda: radiation(prognostic, daylit, cos_zenith, albedo, optics),
    )
    heat_in = lax.ppermute(heat, "grp", [(1, 0)])
    fields = lax.cond(
        dynamics,
        lambda left, right: pass_two(first, prognostic, courant, left, right),
        lambda left, right: expand(daylit, heat, fluxes, prognostic.shape),
        left, right,
    )
    return warm(fields, heat_in)[None]


def solution(mesh):
    column = P("tile")
    plane = P(None, None, "tile", None)
    return jax.shard_map(
        per_device,
        mesh=mesh,
        in_specs=(plane, plane, column, column, column) + (P(),) * 6,
        out_specs=P("grp", None, None, "tile", None),
        check_vma=False,
    )
```

time: 64.9 us -> 48.3 us (0.74)
  waiting for transfers between devices: 18.5 us -> 0.01 us
  Pallas kernels: 27.1 us -> 36.1 us
  local copies, waits for them, and re-layouts: 6.74 us -> 0.73 us
  other arithmetic: 1.44 us -> 0 us
    ppermute x1, waiting for transfers between devices: 11.6 us -> 0.01 us  [per_device(): lax.ppermute(to_right, ('grp', 'tile'), [(i, (i + 1) % tiles) for i in ra...]
    pallas_call x1 -> x3, Pallas kernels: 23.6 us -> 32.6 us  [the longest x1 14.5 us: pass_two(): pl.pallas_call(pass_two_kernel, grid=(levels // block,), in_specs=[plane,...]
    ppermute x1, waiting for transfers between devices: 6.97 us -> 0.01 us  [per_device(): heat_in = lax.ppermute(heat, 'grp', [(1, 0)])]
    slice x8 -> x0, local copies, waits for them, and re-layouts: 5.14 us -> none  [the longest x1 4.6 us: edge_rows(): start, inner = (prognostic[:, :, 0], prognostic[:, :, 1])]
    concatenate x2 -> x0, other arithmetic: 0.88 us -> none  [the longest x1 0.83 us: edge_rows(): to_right = jnp.concatenate([end, partial], axis=0)]
    unnamed x25 -> x20, local copies, waits for them, and re-layouts: 1.41 us -> 0.73 us
  transfers between devices with their start and end apart: 3 -> 3, of which waited for: 2 -> 0; matrix products, arithmetic and copies ran while one was open for 2% -> 0% of each run, Pallas kernels for 0% -> 56%
where the time goes in v1:
time: 48.3 us; the launch traced here: 47.6 us
  Pallas kernels  36.1 us (75%)
  starting transfers between devices  10.6 us (22%)
  local copies, waits for them, and re-layouts  0.73 us (2%)
    pallas_call x1, Pallas kernels, pass_two(): pl.pallas_call(pass_two_kernel, grid=(levels // block,), in_specs=[plane,...  14.5 us
    pallas_call x1, Pallas kernels, pass_one(): pl.pallas_call(pass_one_kernel, grid=(levels // block,), in_specs=[plane,...  12.4 us
    ppermute x1, starting transfers between devices, per_device(): lax.ppermute(to_left, ('grp', 'tile'), [((i + 1) % tiles, i) for i in ran...  7.35 us
    pallas_call x1, Pallas kernels, edges(): pl.pallas_call(edges_kernel, grid=(levels // block,), in_specs=[pl.BlockS...  5.75 us
    pallas_call x1, Pallas kernels, warm(): pl.pallas_call(warm_kernel, grid=(levels // block,), in_specs=[spec, pl.B...  3.5 us
    ppermute x1, starting transfers between devices, per_device(): lax.ppermute(to_right, ('grp', 'tile'), [(i, (i + 1) % tiles) for i in ra...  1.92 us
    ppermute x1, starting transfers between devices, per_device(): heat_in = lax.ppermute(heat, 'grp', [(1, 0)])  1.28 us
  transfers between devices with their start and end apart: 3, of which 0 were waited for; matrix products, arithmetic and copies ran while one was open for 0% of the time, Pallas kernels for 56%

profile of v1, /device:TPU:0, one launch (start us, length us, event | category | flops | bytes accessed | tf_op | source)
XLA Modules:
  0.0 47.6 jit_solution(14582154477518226443)
XLA Ops:
  0.0 0.0 copy-start.1
  0.0 0.0 copy-start.9
  0.0 0.0 copy-start.8
  0.0 0.0 copy-start.7
  0.0 0.0 copy-start.6
  0.0 0.0 copy-start.2
  0.0 0.0 copy-start.5
  0.0 0.0 copy-start.4
  0.0 0.0 copy-start.3
  0.1 5.8 %conditional.4 = ((f32[8,64,256]{2,1,0:T(8,128)S(1)}, f32[9,64,256]{2,1,0:T(8,128)S(1)})) conditional(s32[]{:T(128)} %convert_element_type.2, () %tuple.26, (f32[4,64,16,256]{3,2,1,0:T(8,128)}, f32[2,64,16,256]{3,2,1,0:T(8,128)}) %tuple.24), branch_computations={%region_2.0_spmd, %region_3.0_spmd} | conditional | bytes 8 | solution.py:434
  0.1 5.8 %edges.1 = (f32[8,64,256]{2,1,0:T(8,128)S(1)}, f32[9,64,256]{2,1,0:T(8,128)S(1)}) custom-call(f32[4,64,16,256]{3,2,1,0:T(8,128)} %get-tuple-element.64.prog_ref, f32[2,64,16,256]{3,2,1,0:T(8,128)} %get-tuple-element.65.cour_ref), custom_call_target="tpu_custom_call" | custom-call | tf_op jit(solution)/shard_map/cond/branch_1_fun/edges/pallas_call | solution.py:251
  5.8 7.4 %collective-permute-start.1 = (f32[9,64,256]{2,1,0:T(8,128)S(1)}, f32[9,64,256]{2,1,0:T(8,128)S(1)}, u32[]{:S(2)}, u32[]{:S(2)}) collective-permute-start(f32[9,64,256]{2,1,0:T(8,128)S(1)} %get-tuple-element.83), channel_id=1, source_target_pairs={{1,0},{2,1},{3,2},{4,3},{5,4},{6,5},{7,6},{8,7},{9,8},{10,9},{11,1... | collective-permute-start | bytes 1769480 | tf_op jit(solution)/shard_map/ppermute | solution.py:438
  13.2 1.9 %collective-permute-start = (f32[8,64,256]{2,1,0:T(8,128)S(1)}, f32[8,64,256]{2,1,0:T(8,128)S(1)}, u32[]{:S(2)}, u32[]{:S(2)}) collective-permute-start(f32[8,64,256]{2,1,0:T(8,128)S(1)} %get-tuple-element.82), channel_id=1, source_target_pairs={{0,1},{1,2},{2,3},{3,4},{4,5},{5,6},{6,7},{7,8},{8,9},{9,10},{10,1... | collective-permute-start | bytes 1572872 | tf_op jit(solution)/shard_map/ppermute | solution.py:437
  15.1 0.0 copy-done.1
  15.1 0.0 copy-done.9
  15.2 0.0 copy-done.8
  15.2 0.0 copy-done.7
  15.2 0.0 copy-done.6
  15.2 0.0 copy-done.2
  15.2 0.0 copy-done.5
  15.2 0.0 copy-done.4
  15.2 0.0 copy-done.3
  15.2 12.4 %conditional.3 = ((f32[4,64,16,256]{3,2,1,0:T(8,128)}, f32[64,8,128]{2,1,0:T(8,128)}, f32[4,64,8,128]{3,2,1,0:T(8,128)S(1)})) conditional(s32[]{:T(128)} %convert_element_type.2, (s32[1024]{0:T(1024)S(1)}, f32[1024]{0:T(1024)S(1)}, f32[1024]{0:T(1024)S(1)}, f32[64]{0:T(128)S(1)}, f32[64,32]{0,1:T(8,128)S(1)}, /*index=5*/f32[32]{0:T(128)S(1)}, ...), branch_computations={%region_0.0_spmd, %region_1.0_spmd} | conditional | bytes 16392 | solution.py:439
  15.2 12.4 %pass_one.1 = (f32[4,64,16,256]{3,2,1,0:T(8,128)}, f32[64,8,128]{2,1,0:T(8,128)}, f32[4,64,8,128]{3,2,1,0:T(8,128)S(1)}) custom-call(f32[4,64,16,256]{3,2,1,0:T(8,128)} %get-tuple-element.62.prog_ref, f32[2,64,16,256]{3,2,1,0:T(8,128)} %get-tuple-element.63.cour_ref), custom_call_target="tpu_custom_call" | custom-call | tf_op jit(solution)/shard_map/cond/branch_1_fun/pass_one/pallas_call | solution.py:313
  27.6 1.3 %collective-permute-start.2 = (f32[64,8,128]{2,1,0:T(8,128)}, f32[64,8,128]{2,1,0:T(8,128)S(1)}, u32[]{:S(2)}, u32[]{:S(2)}) collective-permute-start(f32[64,8,128]{2,1,0:T(8,128)} %get-tuple-element.79), channel_id=1, source_target_pairs={{16,0},{17,1},{18,2},{19,3},{20,4},{21,5},{22,6},{23,7},{24,8},{25... | collective-permute-start | bytes 786440 | tf_op jit(solution)/shard_map/ppermute | solution.py:444
  28.9 0.0 collective-permute-done
  28.9 0.0 collective-permute-done.1
  28.9 14.5 %conditional.5 = (f32[4,64,16,256]{3,2,1,0:T(8,128)}) conditional(s32[]{:T(128)} %convert_element_type.2, (s32[1024]{0:T(1024)S(1)}, f32[64,8,128]{2,1,0:T(8,128)}, f32[4,64,8,128]{3,2,1,0:T(8,128)S(1)}) %tuple.40, (f32[4,64,16,256]{3,2,1,0:T(8,128)}, f32[4,64,16,256]{3,2,1,0:T(8,128)}, f32[2,64,16,256]{3,2,1,0:T(8,128)}, ...), branch_computations={%region_4.0_spmd, %region_5.0_spmd} | conditional | bytes 8 | solution.py:445
  28.9 14.5 %pass_two.1 = f32[4,64,16,256]{3,2,1,0:T(8,128)} custom-call(f32[4,64,16,256]{3,2,1,0:T(8,128)} %get-tuple-element.69.first_ref, f32[4,64,16,256]{3,2,1,0:T(8,128)} %get-tuple-element.70.edge_ref, f32[2,64,16,256]{3,2,1,0:T(8,128)} %get-tuple-element.71.cour_ref, f32[8,64,256]{2,1,0:T(8,128)S(1)} %get-tuple-element.72.left_ref, ...), custom_call_target="tpu_custom_call" | custom-call | tf_op jit(solution)/shard_map/cond/branch_1_fun/pass_two/pallas_call | solution.py:382
  43.4 0.0 collective-permute-done.2.heat_ref
  43.4 0.0 copy-start
  43.4 0.7 %copy-done = f32[64,8,128]{2,1,0:T(8,128)} copy-done((f32[64,8,128]{2,1,0:T(8,128)}, f32[64,8,128]{2,1,0:T(8,128)S(1)}, u32[]{:S(2)}) %copy-start) | copy-done | bytes 262168
  44.1 3.5 %warm.1 = f32[4,64,16,256]{3,2,1,0:T(8,128)} custom-call(f32[4,64,16,256]{3,2,1,0:T(8,128)} %get-tuple-element.122.field_ref, f32[64,8,128]{2,1,0:T(8,128)} %copy-done), custom_call_target="tpu_custom_call", output_to_operand_aliasing={{}: (0, {})} | custom-call | tf_op jit(solution)/shard_map/warm/pallas_call | solution.py:420
Async XLA Ops:
  0.0 15.1 %copy-start.1 = (s32[1024]{0:T(1024)S(1)}, s32[1024]{0:T(1024)}, u32[]{:S(2)}) copy-start(s32[1024]{0:T(1024)} %param.19) | copy-start | bytes 12292
  0.0 15.1 %copy-start.9 = (f32[32]{0:T(128)S(1)}, f32[32]{0:T(128)}, u32[]{:S(2)}) copy-start(f32[32]{0:T(128)} %param.27) | copy-start | bytes 388
  0.0 15.1 %copy-start.8 = (f32[32]{0:T(128)S(1)}, f32[32]{0:T(128)}, u32[]{:S(2)}) copy-start(f32[32]{0:T(128)} %param.26) | copy-start | bytes 388
  0.0 15.2 %copy-start.7 = (f32[32]{0:T(128)S(1)}, f32[32]{0:T(128)}, u32[]{:S(2)}) copy-start(f32[32]{0:T(128)} %param.25) | copy-start | bytes 388
  0.0 15.2 %copy-start.6 = (f32[32]{0:T(128)S(1)}, f32[32]{0:T(128)}, u32[]{:S(2)}) copy-start(f32[32]{0:T(128)} %param.24) | copy-start | bytes 388
  0.0 15.2 %copy-start.2 = (f32[64,32]{0,1:T(8,128)S(1)}, f32[64,32]{0,1:T(8,128)}, u32[]{:S(2)}) copy-start(f32[64,32]{0,1:T(8,128)} %param.23) | copy-start | bytes 24580
  0.0 15.2 %copy-start.5 = (f32[64]{0:T(128)S(1)}, f32[64]{0:T(128)}, u32[]{:S(2)}) copy-start(f32[64]{0:T(128)} %param.22) | copy-start | bytes 772
  0.0 15.2 %copy-start.4 = (f32[1024]{0:T(1024)S(1)}, f32[1024]{0:T(1024)}, u32[]{:S(2)}) copy-start(f32[1024]{0:T(1024)} %param.21) | copy-start | bytes 12292
  0.0 15.2 %copy-start.3 = (f32[1024]{0:T(1024)S(1)}, f32[1024]{0:T(1024)}, u32[]{:S(2)}) copy-start(f32[1024]{0:T(1024)} %param.20) | copy-start | bytes 12292
  5.8 23.1 %collective-permute-start.1 = (f32[9,64,256]{2,1,0:T(8,128)S(1)}, f32[9,64,256]{2,1,0:T(8,128)S(1)}, u32[]{:S(2)}, u32[]{:S(2)}) collective-permute-start(f32[9,64,256]{2,1,0:T(8,128)S(1)} %get-tuple-element.83), channel_id=1, source_target_pairs={{1,0},{2,1},{3,2},{4,3},{5,4},{6,5},{7,6},{8,7},{9,8},{10,9},{11,1... | collective-permute-start | bytes 1769480 | tf_op jit(solution)/shard_map/ppermute | solution.py:438
  13.2 15.7 %collective-permute-start = (f32[8,64,256]{2,1,0:T(8,128)S(1)}, f32[8,64,256]{2,1,0:T(8,128)S(1)}, u32[]{:S(2)}, u32[]{:S(2)}) collective-permute-start(f32[8,64,256]{2,1,0:T(8,128)S(1)} %get-tuple-element.82), channel_id=1, source_target_pairs={{0,1},{1,2},{2,3},{3,4},{4,5},{5,6},{6,7},{7,8},{8,9},{9,10},{10,1... | collective-permute-start | bytes 1572872 | tf_op jit(solution)/shard_map/ppermute | solution.py:437
  27.6 15.8 %collective-permute-start.2 = (f32[64,8,128]{2,1,0:T(8,128)}, f32[64,8,128]{2,1,0:T(8,128)S(1)}, u32[]{:S(2)}, u32[]{:S(2)}) collective-permute-start(f32[64,8,128]{2,1,0:T(8,128)} %get-tuple-element.79), channel_id=1, source_target_pairs={{16,0},{17,1},{18,2},{19,3},{20,4},{21,5},{22,6},{23,7},{24,8},{25... | collective-permute-start | bytes 786440 | tf_op jit(solution)/shard_map/ppermute | solution.py:444
  43.4 0.7 %copy-start = (f32[64,8,128]{2,1,0:T(8,128)}, f32[64,8,128]{2,1,0:T(8,128)S(1)}, u32[]{:S(2)}) copy-start(f32[64,8,128]{2,1,0:T(8,128)S(1)} %collective-permute-done.2.heat_ref) | copy-start | bytes 786436

commit v2 on v1

--- a/solution.py
+++ b/solution.py
@@ -12,8 +12,17 @@
 STEP_LENGTH = 1.0
 LOG2E = 1.4426950408889634
 G_CHUNK = 8
-LEVEL_BLOCK = 8
-VMEM_LIMIT = 56 * 1024 * 1024
+UP_UNROLL = 2
+DOWN_UNROLL = 1
+EDGE_BLOCK = 16
+ONE_BLOCK = 16
+ONE_UNROLL = 4
+TWO_BLOCK = 16
+TWO_UNROLL = 4
+EXPAND_BLOCK = 16
+WARM_BLOCK = 16
+SOLVE_VMEM = 24 * 1024 * 1024
+SMALL_VMEM = 16 * 1024 * 1024
 
 
 def pack_means(tile):
@@ -99,7 +108,7 @@
         return tuple(new_dif), tuple(new_dir)
 
     start = (ground,) * G_CHUNK
-    _, top_dir = lax.fori_loop(0, levels, upward, (start, start))
+    _, top_dir = lax.fori_loop(0, levels, upward, (start, start), unroll=UP_UNROLL)
 
     direct0 = tuple(cosine * sol_s[g0 + j] for j in range(G_CHUNK))
     net0 = tuple(d - t * d for d, t in zip(direct0, top_dir))
@@ -124,7 +133,7 @@
             acc[f, l] += sums[f]
         return tuple(n_direct), tuple(n_diffuse), tuple(n_net)
 
-    lax.fori_loop(0, levels, downward, (direct0, diffuse0, net0))
+    lax.fori_loop(0, levels, downward, (direct0, diffuse0, net0), unroll=DOWN_UNROLL)
 
     @pl.when(chunk == pl.num_programs(0) - 1)
     def _():
@@ -164,7 +173,7 @@
             jax.ShapeDtypeStruct((4, levels, 8, 128), jnp.float32),
         ],
         scratch_shapes=[pltpu.VMEM((3, levels, 8, 128), jnp.float32), kept, kept, kept, kept, kept],
-        compiler_params=pltpu.CompilerParams(vmem_limit_bytes=VMEM_LIMIT),
+        compiler_params=pltpu.CompilerParams(vmem_limit_bytes=SOLVE_VMEM),
         name="radiation",
     )(
         *optics,
@@ -191,7 +200,7 @@
 
 def expand(daylit, heat, fluxes, shape):
     fields, levels, cells_x, cells_y = shape
-    block = LEVEL_BLOCK
+    block = EXPAND_BLOCK
     return pl.pallas_call(
         expand_kernel,
         grid=(levels // block,),
@@ -202,6 +211,7 @@
         ],
         out_specs=pl.BlockSpec((fields, block, cells_x, cells_y), lambda i: (0, i, 0, 0)),
         out_shape=jax.ShapeDtypeStruct(shape, jnp.float32),
+        compiler_params=pltpu.CompilerParams(vmem_limit_bytes=SMALL_VMEM),
         name="expand",
     )(daylit.reshape(8, 128), heat, fluxes)
 
@@ -247,7 +257,7 @@
 
 def edges(prognostic, courant):
     fields, levels, cells_x, cells_y = prognostic.shape
-    block = LEVEL_BLOCK
+    block = EDGE_BLOCK
     return pl.pallas_call(
         edges_kernel,
         grid=(levels // block,),
@@ -264,6 +274,7 @@
             jax.ShapeDtypeStruct((2 * fields + 1, levels, cells_y), jnp.float32),
         ],
         scratch_shapes=[pltpu.VMEM((4 * fields + 5, block, cells_y), jnp.float32)],
+        compiler_params=pltpu.CompilerParams(vmem_limit_bytes=SMALL_VMEM),
         name="edges",
     )(prognostic, courant)
 
@@ -277,6 +288,7 @@
             jax.ShapeDtypeStruct((2 * fields, levels, cells_y), jnp.float32),
             jax.ShapeDtypeStruct((2 * fields + 1, levels, cells_y), jnp.float32),
         ],
+        compiler_params=pltpu.CompilerParams(vmem_limit_bytes=SMALL_VMEM),
         name="no_edges",
     )()
 
@@ -303,12 +315,12 @@
             )
         return c
 
-    lax.fori_loop(0, block, body, 0)
+    lax.fori_loop(0, block, body, 0, unroll=ONE_UNROLL)
 
 
 def pass_one(prognostic, courant):
     fields, levels, cells_x, cells_y = prognostic.shape
-    block = LEVEL_BLOCK
+    block = ONE_BLOCK
     plane = pl.BlockSpec((fields, block, cells_x, cells_y), lambda i: (0, i, 0, 0))
     return pl.pallas_call(
         pass_one_kernel,
@@ -320,12 +332,14 @@
             jax.ShapeDtypeStruct((levels, 8, 128), jnp.float32),
             jax.ShapeDtypeStruct((4, levels, 8, 128), jnp.float32),
         ],
+        compiler_params=pltpu.CompilerParams(vmem_limit_bytes=SMALL_VMEM),
         name="pass_one",
     )(prognostic, courant)
 
 
 def pass_two_kernel(
-    first_ref, edge_ref, cour_ref, left_ref, right_ref, out_ref, rows, row_m1, row_0, row_15, flux_16
+    first_ref, cour_ref, my_right, my_left, left_ref, right_ref,
+    out_ref, row_m1, row_0, row_15, flux_16,
 ):
     fields, block, cells_x, cells_y = first_ref.shape
     shape = (cells_x, cells_y)
@@ -334,21 +348,14 @@
     wall = wall_mask(shape)
     is_first, is_last = row == 0, row == last
 
-    for l in range(block):
-        rows[2 * fields, l : l + 1, :] = cour_ref[0, l, :1, :]
-        for f in range(fields):
-            rows[f, l : l + 1, :] = edge_ref[f, l, :1, :]
-            rows[fields + f, l : l + 1, :] = edge_ref[f, l, last:, :]
-            row_0[f, l : l + 1, :] = first_ref[f, l, :1, :]
-            row_15[f, l : l + 1, :] = first_ref[f, l, last:, :]
-    u0, u16 = rows[2 * fields], right_ref[2 * fields]
+    u0, u16 = my_left[2 * fields], right_ref[2 * fields]
     gain = jnp.abs(u16) - u16 * u16
     for f in range(fields):
-        begin = upwind(left_ref[f], rows[f], u0)
-        end = upwind(rows[fields + f], right_ref[f], u16)
+        begin = upwind(left_ref[f], my_left[f], u0)
+        end = upwind(my_right[f], right_ref[f], u16)
         row_m1[f] = left_ref[fields + f] - begin
-        row_0[f] = row_0[f] + begin
-        lo = row_15[f] - end
+        row_0[f] = my_left[fields + f] + begin
+        lo = my_right[fields + f] - end
         hi = right_ref[fields + f] + end
         row_15[f] = lo
         speed = gain * (hi - lo) * inverse(hi + lo)
@@ -371,12 +378,12 @@
             out_ref[f, l] = p - (beyond - flux) - (pltpu.roll(flux_y, cells_y - 1, 1) - flux_y)
         return c
 
-    lax.fori_loop(0, block, body, 0)
-
-
-def pass_two(first, prognostic, courant, left, right):
+    lax.fori_loop(0, block, body, 0, unroll=TWO_UNROLL)
+
+
+def pass_two(first, courant, my_right, my_left, left, right):
     fields, levels, cells_x, cells_y = first.shape
-    block = LEVEL_BLOCK
+    block = TWO_BLOCK
     plane = pl.BlockSpec((fields, block, cells_x, cells_y), lambda i: (0, i, 0, 0))
     rows = pltpu.VMEM((fields, block, cells_y), jnp.float32)
     return pl.pallas_call(
@@ -384,18 +391,18 @@
         grid=(levels // block,),
         in_specs=[
             plane,
-            plane,
             pl.BlockSpec((2, block, cells_x, cells_y), lambda i: (0, i, 0, 0)),
-            pl.BlockSpec((left.shape[0], block, cells_y), lambda i: (0, i, 0)),
-            pl.BlockSpec((right.shape[0], block, cells_y), lambda i: (0, i, 0)),
+        ]
+        + [
+            pl.BlockSpec((edge.shape[0], block, cells_y), lambda i: (0, i, 0))
+            for edge in (my_right, my_left, left, right)
         ],
         out_specs=plane,
         out_shape=jax.ShapeDtypeStruct(first.shape, jnp.float32),
-        scratch_shapes=[
-            pltpu.VMEM((2 * fields + 1, block, cells_y), jnp.float32), rows, rows, rows, rows,
-        ],
+        scratch_shapes=[rows, rows, rows, rows],
+        compiler_params=pltpu.CompilerParams(vmem_limit_bytes=SMALL_VMEM),
         name="pass_two",
-    )(first, prognostic, courant, left, right)
+    )(first, courant, my_right, my_left, left, right)
 
 
 def warm_kernel(field_ref, heat_ref, out_ref):
@@ -415,7 +422,7 @@
 
 def warm(fields, heat):
     _, levels, cells_x, cells_y = fields.shape
-    block = 16
+    block = WARM_BLOCK
     spec = pl.BlockSpec((1, block, cells_x, cells_y), lambda i: (0, i, 0, 0))
     return pl.pallas_call(
         warm_kernel,
@@ -424,6 +431,7 @@
         out_specs=spec,
         out_shape=jax.ShapeDtypeStruct(fields.shape, jnp.float32),
         input_output_aliases={0: 0},
+        compiler_params=pltpu.CompilerParams(vmem_limit_bytes=SMALL_VMEM),
         name="warm",
     )(fields, heat)
 
@@ -444,7 +452,7 @@
     heat_in = lax.ppermute(heat, "grp", [(1, 0)])
     fields = lax.cond(
         dynamics,
-        lambda left, right: pass_two(first, prognostic, courant, left, right),
+        lambda left, right: pass_two(first, courant, to_right, to_left, left, right),
         lambda left, right: expand(daylit, heat, fluxes, prognostic.shape),
         left, right,
     )

time: 48.3 us -> 38.7 us (0.80)
  Pallas kernels: 36.1 us -> 23.6 us
  waiting for transfers between devices: 0.01 us -> 3.89 us
  local copies, waits for them, and re-layouts: 0.73 us -> 0.04 us
    pallas_call x1, Pallas kernels: 14.5 us -> 8.72 us  [pass_two(): pl.pallas_call(pass_two_kernel, grid=(levels // block,), in_specs=[plane,...]
    pallas_call x1, Pallas kernels: 12.4 us -> 7.54 us  [pass_one(): pl.pallas_call(pass_one_kernel, grid=(levels // block,), in_specs=[plane,...]
    ppermute x1, waiting for transfers between devices: 0.01 us -> 2.33 us  [per_device(): lax.ppermute(to_right, ('grp', 'tile'), [(i, (i + 1) % tiles) for i in ra...]
    pallas_call x1, Pallas kernels: 5.75 us -> 3.9 us  [edges(): pl.pallas_call(edges_kernel, grid=(levels // block,), in_specs=[pl.BlockS...]
    ppermute x1, waiting for transfers between devices: 0.01 us -> 1.55 us  [per_device(): heat_in = lax.ppermute(heat, 'grp', [(1, 0)])]
    unnamed x20 -> x18, local copies, waits for them, and re-layouts: 0.73 us -> 0.04 us
  transfers between devices with their start and end apart: 3 -> 3, of which waited for: 0 -> 2; matrix products, arithmetic and copies ran while one was open for 0% -> 0% of each run, Pallas kernels for 56% -> 43%
where the time goes in v2:
time: 38.7 us; the launch traced here: 38.2 us
  Pallas kernels  23.6 us (61%)
  starting transfers between devices  10.6 us (27%)
  waiting for transfers between devices  3.89 us (10%)
    pallas_call x1, Pallas kernels, pass_two(): pl.pallas_call(pass_two_kernel, grid=(levels // block,), in_specs=[plane,...  8.72 us
    pallas_call x1, Pallas kernels, pass_one(): pl.pallas_call(pass_one_kernel, grid=(levels // block,), in_specs=[plane,...  7.54 us
    ppermute x1, starting transfers between devices, per_device(): lax.ppermute(to_left, ('grp', 'tile'), [((i + 1) % tiles, i) for i in ran...  7.35 us
    pallas_call x1, Pallas kernels, edges(): pl.pallas_call(edges_kernel, grid=(levels // block,), in_specs=[pl.BlockS...  3.9 us
    pallas_call x1, Pallas kernels, warm(): pl.pallas_call(warm_kernel, grid=(levels // block,), in_specs=[spec, pl.B...  3.42 us
    ppermute x1, waiting for transfers between devices, per_device(): lax.ppermute(to_right, ('grp', 'tile'), [(i, (i + 1) % tiles) for i in ra...  2.33 us
    ppermute x1, starting transfers between devices, per_device(): lax.ppermute(to_right, ('grp', 'tile'), [(i, (i + 1) % tiles) for i in ra...  1.92 us
    ppermute x1, waiting for transfers between devices, per_device(): heat_in = lax.ppermute(heat, 'grp', [(1, 0)])  1.55 us
  transfers between devices with their start and end apart: 3, of which 2 were waited for; matrix products, arithmetic and copies ran while one was open for 0% of the time, Pallas kernels for 43%

profile of v2, /device:TPU:0, one launch (start us, length us, event | category | flops | bytes accessed | tf_op | source)
XLA Modules:
  0.0 38.2 jit_solution(2107825879951454225)
XLA Ops:
  0.0 0.0 copy-start
  0.0 0.0 copy-start.8
  0.0 0.0 copy-start.7
  0.0 0.0 copy-start.6
  0.0 0.0 copy-start.5
  0.0 0.0 copy-start.1
  0.0 0.0 copy-start.4
  0.0 0.0 copy-start.3
  0.0 0.0 copy-start.2
  0.1 3.9 %conditional.4 = ((f32[8,64,256]{2,1,0:T(8,128)S(1)}, f32[9,64,256]{2,1,0:T(8,128)S(1)})) conditional(s32[]{:T(128)} %convert_element_type.2, () %tuple.26, (f32[4,64,16,256]{3,2,1,0:T(8,128)}, f32[2,64,16,256]{3,2,1,0:T(8,128)}) %tuple.24), branch_computations={%region_2.0_spmd, %region_3.0_spmd} | conditional | bytes 8 | solution.py:442
  0.1 3.9 %edges.1 = (f32[8,64,256]{2,1,0:T(8,128)S(1)}, f32[9,64,256]{2,1,0:T(8,128)S(1)}) custom-call(f32[4,64,16,256]{3,2,1,0:T(8,128)} %get-tuple-element.66.prog_ref, f32[2,64,16,256]{3,2,1,0:T(8,128)} %get-tuple-element.67.cour_ref), custom_call_target="tpu_custom_call" | custom-call | tf_op jit(solution)/shard_map/cond/branch_1_fun/edges/pallas_call | solution.py:261
  4.0 7.4 %collective-permute-start.1 = (f32[9,64,256]{2,1,0:T(8,128)S(1)}, f32[9,64,256]{2,1,0:T(8,128)S(1)}, u32[]{:S(2)}, u32[]{:S(2)}) collective-permute-start(f32[9,64,256]{2,1,0:T(8,128)S(1)} %get-tuple-element.86), channel_id=1, source_target_pairs={{1,0},{2,1},{3,2},{4,3},{5,4},{6,5},{7,6},{8,7},{9,8},{10,9},{11,1... | collective-permute-start | bytes 1769480 | tf_op jit(solution)/shard_map/ppermute | solution.py:446
  11.3 1.9 %collective-permute-start = (f32[8,64,256]{2,1,0:T(8,128)S(1)}, f32[8,64,256]{2,1,0:T(8,128)S(1)}, u32[]{:S(2)}, u32[]{:S(2)}) collective-permute-start(f32[8,64,256]{2,1,0:T(8,128)S(1)} %get-tuple-element.85), channel_id=1, source_target_pairs={{0,1},{1,2},{2,3},{3,4},{4,5},{5,6},{6,7},{7,8},{8,9},{9,10},{10,1... | collective-permute-start | bytes 1572872 | tf_op jit(solution)/shard_map/ppermute | solution.py:445
  13.3 0.0 copy-done
  13.3 0.0 copy-done.8
  13.3 0.0 copy-done.7
  13.3 0.0 copy-done.6
  13.3 0.0 copy-done.5
  13.3 0.0 copy-done.1
  13.3 0.0 copy-done.4
  13.3 0.0 copy-done.3
  13.4 0.0 copy-done.2
  13.4 7.6 %conditional.3 = ((f32[4,64,16,256]{3,2,1,0:T(8,128)}, f32[64,8,128]{2,1,0:T(8,128)}, f32[4,64,8,128]{3,2,1,0:T(8,128)S(1)})) conditional(s32[]{:T(128)} %convert_element_type.2, (s32[1024]{0:T(1024)S(1)}, f32[1024]{0:T(1024)S(1)}, f32[1024]{0:T(1024)S(1)}, f32[64]{0:T(128)S(1)}, f32[64,32]{0,1:T(8,128)S(1)}, /*index=5*/f32[32]{0:T(128)S(1)}, ...), branch_computations={%region_0.0_spmd, %region_1.0_spmd} | conditional | bytes 16392 | solution.py:447
  13.4 7.5 %pass_one.1 = (f32[4,64,16,256]{3,2,1,0:T(8,128)}, f32[64,8,128]{2,1,0:T(8,128)}, f32[4,64,8,128]{3,2,1,0:T(8,128)S(1)}) custom-call(f32[4,64,16,256]{3,2,1,0:T(8,128)} %get-tuple-element.64.prog_ref, f32[2,64,16,256]{3,2,1,0:T(8,128)} %get-tuple-element.65.cour_ref), custom_call_target="tpu_custom_call" | custom-call | tf_op jit(solution)/shard_map/cond/branch_1_fun/pass_one/pallas_call | solution.py:325
  20.9 1.3 %collective-permute-start.2 = (f32[64,8,128]{2,1,0:T(8,128)}, f32[64,8,128]{2,1,0:T(8,128)S(1)}, u32[]{:S(2)}, u32[]{:S(2)}) collective-permute-start(f32[64,8,128]{2,1,0:T(8,128)} %get-tuple-element.82), channel_id=1, source_target_pairs={{16,0},{17,1},{18,2},{19,3},{20,4},{21,5},{22,6},{23,7},{24,8},{25... | collective-permute-start | bytes 786440 | tf_op jit(solution)/shard_map/ppermute | solution.py:452
  22.2 2.3 %collective-permute-done = f32[8,64,256]{2,1,0:T(8,128)S(1)} collective-permute-done((f32[8,64,256]{2,1,0:T(8,128)S(1)}, f32[8,64,256]{2,1,0:T(8,128)S(1)}, u32[]{:S(2)}, u32[]{:S(2)}) %collective-permute-start) | collective-permute-done | bytes 524320 | tf_op jit(solution)/shard_map/ppermute | solution.py:445
  24.5 0.0 collective-permute-done.1
  24.5 8.7 %conditional.5 = (f32[4,64,16,256]{3,2,1,0:T(8,128)}) conditional(s32[]{:T(128)} %convert_element_type.2, (s32[1024]{0:T(1024)S(1)}, f32[64,8,128]{2,1,0:T(8,128)}, f32[4,64,8,128]{3,2,1,0:T(8,128)S(1)}) %tuple.40, (f32[4,64,16,256]{3,2,1,0:T(8,128)}, f32[2,64,16,256]{3,2,1,0:T(8,128)}, f32[8,64,256]{2,1,0:T(8,128)S(1)}, f32[9,64,256]{2,1,0:T(8,128)S(1)}, ...), branch_computations={%region_4.0_spmd, %region_5.0_spmd} | conditional | bytes 8 | solution.py:453
  24.5 8.7 %pass_two.1 = f32[4,64,16,256]{3,2,1,0:T(8,128)} custom-call(f32[4,64,16,256]{3,2,1,0:T(8,128)} %get-tuple-element.71.first_ref, f32[2,64,16,256]{3,2,1,0:T(8,128)} %get-tuple-element.72.cour_ref, f32[8,64,256]{2,1,0:T(8,128)S(1)} %get-tuple-element.73.my_right, f32[9,64,256]{2,1,0:T(8,128)S(1)} %get-tuple-element.74.my_left, ...), custom_call_target="tpu_custom_call" | custom-call | tf_op jit(solution)/shard_map/cond/branch_1_fun/pass_two/pallas_call | solution.py:389
  33.3 1.6 %collective-permute-done.2.heat_ref = f32[64,8,128]{2,1,0:T(8,128)S(1)} collective-permute-done((f32[64,8,128]{2,1,0:T(8,128)}, f32[64,8,128]{2,1,0:T(8,128)S(1)}, u32[]{:S(2)}, u32[]{:S(2)}) %collective-permute-start.2) | collective-permute-done | bytes 262176 | tf_op jit(solution)/shard_map/ppermute | solution.py:452
  34.8 3.4 %warm.1 = f32[4,64,16,256]{3,2,1,0:T(8,128)} custom-call(f32[4,64,16,256]{3,2,1,0:T(8,128)} %get-tuple-element.125.field_ref, f32[64,8,128]{2,1,0:T(8,128)S(1)} %collective-permute-done.2.heat_ref), custom_call_target="tpu_custom_call", output_to_operand_aliasing={{}: (0, {})} | custom-call | tf_op jit(solution)/shard_map/warm/pallas_call | solution.py:427
Async XLA Ops:
  0.0 13.3 %copy-start = (s32[1024]{0:T(1024)S(1)}, s32[1024]{0:T(1024)}, u32[]{:S(2)}) copy-start(s32[1024]{0:T(1024)} %param.19) | copy-start | bytes 12292
  0.0 13.3 %copy-start.8 = (f32[32]{0:T(128)S(1)}, f32[32]{0:T(128)}, u32[]{:S(2)}) copy-start(f32[32]{0:T(128)} %param.27) | copy-start | bytes 388
  0.0 13.3 %copy-start.7 = (f32[32]{0:T(128)S(1)}, f32[32]{0:T(128)}, u32[]{:S(2)}) copy-start(f32[32]{0:T(128)} %param.26) | copy-start | bytes 388
  0.0 13.3 %copy-start.6 = (f32[32]{0:T(128)S(1)}, f32[32]{0:T(128)}, u32[]{:S(2)}) copy-start(f32[32]{0:T(128)} %param.25) | copy-start | bytes 388
  0.0 13.3 %copy-start.5 = (f32[32]{0:T(128)S(1)}, f32[32]{0:T(128)}, u32[]{:S(2)}) copy-start(f32[32]{0:T(128)} %param.24) | copy-start | bytes 388
  0.0 13.3 %copy-start.1 = (f32[64,32]{0,1:T(8,128)S(1)}, f32[64,32]{0,1:T(8,128)}, u32[]{:S(2)}) copy-start(f32[64,32]{0,1:T(8,128)} %param.23) | copy-start | bytes 24580
  0.0 13.3 %copy-start.4 = (f32[64]{0:T(128)S(1)}, f32[64]{0:T(128)}, u32[]{:S(2)}) copy-start(f32[64]{0:T(128)} %param.22) | copy-start | bytes 772
  0.0 13.3 %copy-start.3 = (f32[1024]{0:T(1024)S(1)}, f32[1024]{0:T(1024)}, u32[]{:S(2)}) copy-start(f32[1024]{0:T(1024)} %param.21) | copy-start | bytes 12292
  0.0 13.3 %copy-start.2 = (f32[1024]{0:T(1024)S(1)}, f32[1024]{0:T(1024)}, u32[]{:S(2)}) copy-start(f32[1024]{0:T(1024)} %param.20) | copy-start | bytes 12292
  4.0 20.6 %collective-permute-start.1 = (f32[9,64,256]{2,1,0:T(8,128)S(1)}, f32[9,64,256]{2,1,0:T(8,128)S(1)}, u32[]{:S(2)}, u32[]{:S(2)}) collective-permute-start(f32[9,64,256]{2,1,0:T(8,128)S(1)} %get-tuple-element.86), channel_id=1, source_target_pairs={{1,0},{2,1},{3,2},{4,3},{5,4},{6,5},{7,6},{8,7},{9,8},{10,9},{11,1... | collective-permute-start | bytes 1769480 | tf_op jit(solution)/shard_map/ppermute | solution.py:446
  11.3 13.2 %collective-permute-start = (f32[8,64,256]{2,1,0:T(8,128)S(1)}, f32[8,64,256]{2,1,0:T(8,128)S(1)}, u32[]{:S(2)}, u32[]{:S(2)}) collective-permute-start(f32[8,64,256]{2,1,0:T(8,128)S(1)} %get-tuple-element.85), channel_id=1, source_target_pairs={{0,1},{1,2},{2,3},{3,4},{4,5},{5,6},{6,7},{7,8},{8,9},{9,10},{10,1... | collective-permute-start | bytes 1572872 | tf_op jit(solution)/shard_map/ppermute | solution.py:445
  20.9 13.9 %collective-permute-start.2 = (f32[64,8,128]{2,1,0:T(8,128)}, f32[64,8,128]{2,1,0:T(8,128)S(1)}, u32[]{:S(2)}, u32[]{:S(2)}) collective-permute-start(f32[64,8,128]{2,1,0:T(8,128)} %get-tuple-element.82), channel_id=1, source_target_pairs={{16,0},{17,1},{18,2},{19,3},{20,4},{21,5},{22,6},{23,7},{24,8},{25... | collective-permute-start | bytes 786440 | tf_op jit(solution)/shard_map/ppermute | solution.py:452

commit v3 on v2

--- a/solution.py
+++ b/solution.py
@@ -20,7 +20,10 @@
 TWO_BLOCK = 16
 TWO_UNROLL = 4
 EXPAND_BLOCK = 16
-WARM_BLOCK = 16
+WARM_BLOCK = 32
+WARM_UNROLL = 8
+COARSE_UNROLL = 8
+COARSE_CHUNKS = 4
 SOLVE_VMEM = 24 * 1024 * 1024
 SMALL_VMEM = 16 * 1024 * 1024
 
@@ -47,30 +50,48 @@
     return jnp.where(lax.broadcasted_iota(jnp.int32, (8, 128), 0) < 4, low, high)
 
 
+def spread_row(ref, l, xh, yh):
+    k = 2 * xh + yh
+    low = jnp.broadcast_to(ref[l, k : k + 1, :], (8, 128))
+    high = jnp.broadcast_to(ref[l, 4 + k : 5 + k, :], (8, 128))
+    return jnp.where(lax.broadcasted_iota(jnp.int32, (8, 128), 0) < 4, low, high)
+
+
 def register_order(rows):
     return jnp.concatenate([rows[0:2], rows[4:6], rows[2:4], rows[6:8]], axis=0)
 
 
 def radiation_kernel(
     mass_s, vap_s, oz_s, ext_s, alb_s, sol_s,
-    lit_ref, cos_ref, ground_ref, vapour_ref, cloud_ref, ozone_ref,
+    lit_ref, cos_ref, ground_ref, prog_ref,
     unused_ref, heat_ref, acc,
-    coarse, k_tdir, k_a, k_b, k_ad, k_as,
+    fine, sems, coarse, k_tdir, k_a, k_b, k_ad, k_as,
 ):
     chunk = pl.program_id(0)
     levels = acc.shape[1]
 
     @pl.when(chunk == 0)
     def _():
+        part = levels // COARSE_CHUNKS
+        copies = []
+        for c in range(COARSE_CHUNKS):
+            here = pl.ds(c * part, part)
+            copies.append(
+                pltpu.make_async_copy(prog_ref.at[pl.ds(1, 3), here], fine.at[:, here], sems.at[c])
+            )
+            copies[-1].start()
+
         def body(l, c):
             scale = mass_s[l]
-            for f, ref in enumerate((vapour_ref, cloud_ref, ozone_ref)):
-                coarse[f, l] = pack_means(ref[0, l]) * scale
+            for f in range(3):
+                coarse[f, l] = pack_means(fine[f, l]) * scale
             for f in range(4):
                 acc[f, l] = jnp.zeros((8, 128), jnp.float32)
             return c
 
-        lax.fori_loop(0, levels, body, 0, unroll=2)
+        for c in range(COARSE_CHUNKS):
+            copies[c].wait()
+            lax.fori_loop(c * part, (c + 1) * part, body, 0, unroll=COARSE_UNROLL)
 
     cosine = register_order(cos_ref[...])
     ground = register_order(ground_ref[...])
@@ -151,17 +172,11 @@
     g_points = optics[1].shape[1]
     smem = pl.BlockSpec(memory_space=pltpu.SMEM)
     vec = pl.BlockSpec((8, 128), lambda c: (0, 0))
-    field_specs = [
-        pl.BlockSpec(
-            (1, levels, cells_x, cells_y), lambda c, f=f: (f, 0, 0, 0), pipeline_mode=pl.Buffered(1)
-        )
-        for f in range(1, 4)
-    ]
     kept = pltpu.VMEM((levels, G_CHUNK, 8, 128), jnp.float32)
     return pl.pallas_call(
         radiation_kernel,
         grid=(g_points // G_CHUNK,),
-        in_specs=[smem] * 6 + [vec] * 3 + field_specs,
+        in_specs=[smem] * 6 + [vec] * 3 + [pl.BlockSpec(memory_space=pl.ANY)],
         out_specs=[
             pl.BlockSpec(memory_space=pl.ANY),
             pl.BlockSpec((levels, 8, 128), lambda c: (0, 0, 0)),
@@ -172,13 +187,18 @@
             jax.ShapeDtypeStruct((levels, 8, 128), jnp.float32),
             jax.ShapeDtypeStruct((4, levels, 8, 128), jnp.float32),
         ],
-        scratch_shapes=[pltpu.VMEM((3, levels, 8, 128), jnp.float32), kept, kept, kept, kept, kept],
+        scratch_shapes=[
+            pltpu.VMEM((3, levels, cells_x, cells_y), jnp.float32),
+            pltpu.SemaphoreType.DMA((COARSE_CHUNKS,)),
+            pltpu.VMEM((3, levels, 8, 128), jnp.float32),
+            kept, kept, kept, kept, kept,
+        ],
         compiler_params=pltpu.CompilerParams(vmem_limit_bytes=SOLVE_VMEM),
         name="radiation",
     )(
         *optics,
         daylit.reshape(8, 128), cos_zenith.reshape(8, 128), albedo.reshape(8, 128),
-        prognostic, prognostic, prognostic,
+        prognostic,
     )
 
 
@@ -410,14 +430,14 @@
     start = pl.program_id(0) * block
 
     def body(l, c):
-        packed = heat_ref[start + l] * STEP_LENGTH
         for xh in range(2):
             for yh in range(2):
                 part = (0, l, slice(8 * xh, 8 * xh + 8), slice(128 * yh, 128 * yh + 128))
-                out_ref[part] = field_ref[part] + spread_part(packed, xh, yh)
+                heating = spread_row(heat_ref, start + l, xh, yh)
+                out_ref[part] = field_ref[part] + STEP_LENGTH * heating
         return c
 
-    lax.fori_loop(0, block, body, 0, unroll=4)
+    lax.fori_loop(0, block, body, 0, unroll=WARM_UNROLL)
 
 
 def warm(fields, heat):

time: 38.7 us -> 37.7 us (0.974)
  Pallas kernels: 23.6 us -> 22.2 us
  waiting for transfers between devices: 3.89 us -> 4.33 us
    pallas_call x1, Pallas kernels: 3.42 us -> 2.09 us  [warm(): pl.pallas_call(warm_kernel, grid=(levels // block,), in_specs=[spec, pl.B...]
    ppermute x1, waiting for transfers between devices: 1.55 us -> 1.99 us  [per_device(): heat_in = lax.ppermute(heat, 'grp', [(1, 0)])]
where the time goes in v3:
time: 37.7 us; the launch traced here: 37.4 us
  Pallas kernels  22.2 us (59%)
  starting transfers between devices  10.6 us (28%)
  waiting for transfers between devices  4.33 us (11%)
    pallas_call x1, Pallas kernels, pass_two(): pl.pallas_call(pass_two_kernel, grid=(levels // block,), in_specs=[plane,...  8.72 us
    pallas_call x1, Pallas kernels, pass_one(): pl.pallas_call(pass_one_kernel, grid=(levels // block,), in_specs=[plane,...  7.54 us
    ppermute x1, starting transfers between devices, per_device(): lax.ppermute(to_left, ('grp', 'tile'), [((i + 1) % tiles, i) for i in ran...  7.35 us
    pallas_call x1, Pallas kernels, edges(): pl.pallas_call(edges_kernel, grid=(levels // block,), in_specs=[pl.BlockS...  3.9 us
    ppermute x1, waiting for transfers between devices, per_device(): lax.ppermute(to_right, ('grp', 'tile'), [(i, (i + 1) % tiles) for i in ra...  2.33 us
    pallas_call x1, Pallas kernels, warm(): pl.pallas_call(warm_kernel, grid=(levels // block,), in_specs=[spec, pl.B...  2.09 us
    ppermute x1, waiting for transfers between devices, per_device(): heat_in = lax.ppermute(heat, 'grp', [(1, 0)])  1.99 us
    ppermute x1, starting transfers between devices, per_device(): lax.ppermute(to_right, ('grp', 'tile'), [(i, (i + 1) % tiles) for i in ra...  1.92 us
  transfers between devices with their start and end apart: 3, of which 2 were waited for; matrix products, arithmetic and copies ran while one was open for 0% of the time, Pallas kernels for 43%

profile of v3, /device:TPU:0, one launch (start us, length us, event | category | flops | bytes accessed | tf_op | source)
XLA Modules:
  0.0 37.4 jit_solution(16415560129746941914)
XLA Ops:
  0.0 0.0 copy-start
  0.0 0.0 copy-start.8
  0.0 0.0 copy-start.7
  0.0 0.0 copy-start.6
  0.0 0.0 copy-start.5
  0.0 0.0 copy-start.1
  0.0 0.0 copy-start.4
  0.0 0.0 copy-start.3
  0.0 0.0 copy-start.2
  0.1 3.9 %conditional.4 = ((f32[8,64,256]{2,1,0:T(8,128)S(1)}, f32[9,64,256]{2,1,0:T(8,128)S(1)})) conditional(s32[]{:T(128)} %convert_element_type.2, () %tuple.26, (f32[4,64,16,256]{3,2,1,0:T(8,128)}, f32[2,64,16,256]{3,2,1,0:T(8,128)}) %tuple.24), branch_computations={%region_2.0_spmd, %region_3.0_spmd} | conditional | bytes 8 | solution.py:462
  0.1 3.9 %edges.1 = (f32[8,64,256]{2,1,0:T(8,128)S(1)}, f32[9,64,256]{2,1,0:T(8,128)S(1)}) custom-call(f32[4,64,16,256]{3,2,1,0:T(8,128)} %get-tuple-element.66.prog_ref, f32[2,64,16,256]{3,2,1,0:T(8,128)} %get-tuple-element.67.cour_ref), custom_call_target="tpu_custom_call" | custom-call | tf_op jit(solution)/shard_map/cond/branch_1_fun/edges/pallas_call | solution.py:281
  4.0 7.4 %collective-permute-start.1 = (f32[9,64,256]{2,1,0:T(8,128)S(1)}, f32[9,64,256]{2,1,0:T(8,128)S(1)}, u32[]{:S(2)}, u32[]{:S(2)}) collective-permute-start(f32[9,64,256]{2,1,0:T(8,128)S(1)} %get-tuple-element.86), channel_id=1, source_target_pairs={{1,0},{2,1},{3,2},{4,3},{5,4},{6,5},{7,6},{8,7},{9,8},{10,9},{11,1... | collective-permute-start | bytes 1769480 | tf_op jit(solution)/shard_map/ppermute | solution.py:466
  11.3 1.9 %collective-permute-start = (f32[8,64,256]{2,1,0:T(8,128)S(1)}, f32[8,64,256]{2,1,0:T(8,128)S(1)}, u32[]{:S(2)}, u32[]{:S(2)}) collective-permute-start(f32[8,64,256]{2,1,0:T(8,128)S(1)} %get-tuple-element.85), channel_id=1, source_target_pairs={{0,1},{1,2},{2,3},{3,4},{4,5},{5,6},{6,7},{7,8},{8,9},{9,10},{10,1... | collective-permute-start | bytes 1572872 | tf_op jit(solution)/shard_map/ppermute | solution.py:465
  13.3 0.0 copy-done
  13.3 0.0 copy-done.8
  13.3 0.0 copy-done.7
  13.3 0.0 copy-done.6
  13.3 0.0 copy-done.5
  13.3 0.0 copy-done.1
  13.3 0.0 copy-done.4
  13.3 0.0 copy-done.3
  13.4 0.0 copy-done.2
  13.4 7.6 %conditional.3 = ((f32[4,64,16,256]{3,2,1,0:T(8,128)}, f32[64,8,128]{2,1,0:T(8,128)}, f32[4,64,8,128]{3,2,1,0:T(8,128)S(1)})) conditional(s32[]{:T(128)} %convert_element_type.2, (s32[1024]{0:T(1024)S(1)}, f32[1024]{0:T(1024)S(1)}, f32[1024]{0:T(1024)S(1)}, f32[64]{0:T(128)S(1)}, f32[64,32]{0,1:T(8,128)S(1)}, /*index=5*/f32[32]{0:T(128)S(1)}, ...), branch_computations={%region_0.0_spmd, %region_1.0_spmd} | conditional | bytes 16392 | solution.py:467
  13.4 7.5 %pass_one.1 = (f32[4,64,16,256]{3,2,1,0:T(8,128)}, f32[64,8,128]{2,1,0:T(8,128)}, f32[4,64,8,128]{3,2,1,0:T(8,128)S(1)}) custom-call(f32[4,64,16,256]{3,2,1,0:T(8,128)} %get-tuple-element.64.prog_ref, f32[2,64,16,256]{3,2,1,0:T(8,128)} %get-tuple-element.65.cour_ref), custom_call_target="tpu_custom_call" | custom-call | tf_op jit(solution)/shard_map/cond/branch_1_fun/pass_one/pallas_call | solution.py:345
  20.9 1.3 %collective-permute-start.2 = (f32[64,8,128]{2,1,0:T(8,128)}, f32[64,8,128]{2,1,0:T(8,128)S(1)}, u32[]{:S(2)}, u32[]{:S(2)}) collective-permute-start(f32[64,8,128]{2,1,0:T(8,128)} %get-tuple-element.82), channel_id=1, source_target_pairs={{16,0},{17,1},{18,2},{19,3},{20,4},{21,5},{22,6},{23,7},{24,8},{25... | collective-permute-start | bytes 786440 | tf_op jit(solution)/shard_map/ppermute | solution.py:472
  22.2 2.3 %collective-permute-done = f32[8,64,256]{2,1,0:T(8,128)S(1)} collective-permute-done((f32[8,64,256]{2,1,0:T(8,128)S(1)}, f32[8,64,256]{2,1,0:T(8,128)S(1)}, u32[]{:S(2)}, u32[]{:S(2)}) %collective-permute-start) | collective-permute-done | bytes 524320 | tf_op jit(solution)/shard_map/ppermute | solution.py:465
  24.5 0.0 collective-permute-done.1
  24.5 8.7 %conditional.5 = (f32[4,64,16,256]{3,2,1,0:T(8,128)}) conditional(s32[]{:T(128)} %convert_element_type.2, (s32[1024]{0:T(1024)S(1)}, f32[64,8,128]{2,1,0:T(8,128)}, f32[4,64,8,128]{3,2,1,0:T(8,128)S(1)}) %tuple.40, (f32[4,64,16,256]{3,2,1,0:T(8,128)}, f32[2,64,16,256]{3,2,1,0:T(8,128)}, f32[8,64,256]{2,1,0:T(8,128)S(1)}, f32[9,64,256]{2,1,0:T(8,128)S(1)}, ...), branch_computations={%region_4.0_spmd, %region_5.0_spmd} | conditional | bytes 8 | solution.py:473
  24.5 8.7 %pass_two.1 = f32[4,64,16,256]{3,2,1,0:T(8,128)} custom-call(f32[4,64,16,256]{3,2,1,0:T(8,128)} %get-tuple-element.71.first_ref, f32[2,64,16,256]{3,2,1,0:T(8,128)} %get-tuple-element.72.cour_ref, f32[8,64,256]{2,1,0:T(8,128)S(1)} %get-tuple-element.73.my_right, f32[9,64,256]{2,1,0:T(8,128)S(1)} %get-tuple-element.74.my_left, ...), custom_call_target="tpu_custom_call" | custom-call | tf_op jit(solution)/shard_map/cond/branch_1_fun/pass_two/pallas_call | solution.py:409
  33.3 2.0 %collective-permute-done.2.heat_ref = f32[64,8,128]{2,1,0:T(8,128)S(1)} collective-permute-done((f32[64,8,128]{2,1,0:T(8,128)}, f32[64,8,128]{2,1,0:T(8,128)S(1)}, u32[]{:S(2)}, u32[]{:S(2)}) %collective-permute-start.2) | collective-permute-done | bytes 262176 | tf_op jit(solution)/shard_map/ppermute | solution.py:472
  35.3 2.1 %warm.1 = f32[4,64,16,256]{3,2,1,0:T(8,128)} custom-call(f32[4,64,16,256]{3,2,1,0:T(8,128)} %get-tuple-element.125.field_ref, f32[64,8,128]{2,1,0:T(8,128)S(1)} %collective-permute-done.2.heat_ref), custom_call_target="tpu_custom_call", output_to_operand_aliasing={{}: (0, {})} | custom-call | tf_op jit(solution)/shard_map/warm/pallas_call | solution.py:447
Async XLA Ops:
  0.0 13.3 %copy-start = (s32[1024]{0:T(1024)S(1)}, s32[1024]{0:T(1024)}, u32[]{:S(2)}) copy-start(s32[1024]{0:T(1024)} %param.19) | copy-start | bytes 12292
  0.0 13.3 %copy-start.8 = (f32[32]{0:T(128)S(1)}, f32[32]{0:T(128)}, u32[]{:S(2)}) copy-start(f32[32]{0:T(128)} %param.27) | copy-start | bytes 388
  0.0 13.3 %copy-start.7 = (f32[32]{0:T(128)S(1)}, f32[32]{0:T(128)}, u32[]{:S(2)}) copy-start(f32[32]{0:T(128)} %param.26) | copy-start | bytes 388
  0.0 13.3 %copy-start.6 = (f32[32]{0:T(128)S(1)}, f32[32]{0:T(128)}, u32[]{:S(2)}) copy-start(f32[32]{0:T(128)} %param.25) | copy-start | bytes 388
  0.0 13.3 %copy-start.5 = (f32[32]{0:T(128)S(1)}, f32[32]{0:T(128)}, u32[]{:S(2)}) copy-start(f32[32]{0:T(128)} %param.24) | copy-start | bytes 388
  0.0 13.3 %copy-start.1 = (f32[64,32]{0,1:T(8,128)S(1)}, f32[64,32]{0,1:T(8,128)}, u32[]{:S(2)}) copy-start(f32[64,32]{0,1:T(8,128)} %param.23) | copy-start | bytes 24580
  0.0 13.3 %copy-start.4 = (f32[64]{0:T(128)S(1)}, f32[64]{0:T(128)}, u32[]{:S(2)}) copy-start(f32[64]{0:T(128)} %param.22) | copy-start | bytes 772
  0.0 13.3 %copy-start.3 = (f32[1024]{0:T(1024)S(1)}, f32[1024]{0:T(1024)}, u32[]{:S(2)}) copy-start(f32[1024]{0:T(1024)} %param.21) | copy-start | bytes 12292
  0.0 13.3 %copy-start.2 = (f32[1024]{0:T(1024)S(1)}, f32[1024]{0:T(1024)}, u32[]{:S(2)}) copy-start(f32[1024]{0:T(1024)} %param.20) | copy-start | bytes 12292
  4.0 20.6 %collective-permute-start.1 = (f32[9,64,256]{2,1,0:T(8,128)S(1)}, f32[9,64,256]{2,1,0:T(8,128)S(1)}, u32[]{:S(2)}, u32[]{:S(2)}) collective-permute-start(f32[9,64,256]{2,1,0:T(8,128)S(1)} %get-tuple-element.86), channel_id=1, source_target_pairs={{1,0},{2,1},{3,2},{4,3},{5,4},{6,5},{7,6},{8,7},{9,8},{10,9},{11,1... | collective-permute-start | bytes 1769480 | tf_op jit(solution)/shard_map/ppermute | solution.py:466
  11.3 13.2 %collective-permute-start = (f32[8,64,256]{2,1,0:T(8,128)S(1)}, f32[8,64,256]{2,1,0:T(8,128)S(1)}, u32[]{:S(2)}, u32[]{:S(2)}) collective-permute-start(f32[8,64,256]{2,1,0:T(8,128)S(1)} %get-tuple-element.85), channel_id=1, source_target_pairs={{0,1},{1,2},{2,3},{3,4},{4,5},{5,6},{6,7},{7,8},{8,9},{9,10},{10,1... | collective-permute-start | bytes 1572872 | tf_op jit(solution)/shard_map/ppermute | solution.py:465
  20.9 14.3 %collective-permute-start.2 = (f32[64,8,128]{2,1,0:T(8,128)}, f32[64,8,128]{2,1,0:T(8,128)S(1)}, u32[]{:S(2)}, u32[]{:S(2)}) collective-permute-start(f32[64,8,128]{2,1,0:T(8,128)} %get-tuple-element.82), channel_id=1, source_target_pairs={{16,0},{17,1},{18,2},{19,3},{20,4},{21,5},{22,6},{23,7},{24,8},{25... | collective-permute-start | bytes 786440 | tf_op jit(solution)/shard_map/ppermute | solution.py:472

commit v4 on v3

--- a/solution.py
+++ b/solution.py
@@ -12,9 +12,9 @@
 STEP_LENGTH = 1.0
 LOG2E = 1.4426950408889634
 G_CHUNK = 8
-UP_UNROLL = 2
-DOWN_UNROLL = 1
-EDGE_BLOCK = 16
+UP_UNROLL = 4
+DOWN_UNROLL = 4
+EDGE_BLOCK = 32
 ONE_BLOCK = 16
 ONE_UNROLL = 4
 TWO_BLOCK = 16

time: 37.7 us -> 35.6 us (0.944)
  waiting for transfers between devices: 4.33 us -> 2.7 us
  Pallas kernels: 22.2 us -> 21.7 us
    ppermute x1, waiting for transfers between devices: 1.99 us -> 0.36 us  [per_device(): heat_in = lax.ppermute(heat, 'grp', [(1, 0)])]
    pallas_call x1, Pallas kernels: 3.9 us -> 3.4 us  [edges(): pl.pallas_call(edges_kernel, grid=(levels // block,), in_specs=[pl.BlockS...]
  transfers between devices with their start and end apart: 3 -> 3, of which waited for: 2 -> 2; matrix products, arithmetic and copies ran while one was open for 0% -> 0% of each run, Pallas kernels for 43% -> 46%
where the time goes in v4:
time: 35.6 us; the launch traced here: 35.2 us
  Pallas kernels  21.7 us (61%)
  starting transfers between devices  10.6 us (30%)
  waiting for transfers between devices  2.7 us (8%)
    pallas_call x1, Pallas kernels, pass_two(): pl.pallas_call(pass_two_kernel, grid=(levels // block,), in_specs=[plane,...  8.72 us
    pallas_call x1, Pallas kernels, pass_one(): pl.pallas_call(pass_one_kernel, grid=(levels // block,), in_specs=[plane,...  7.54 us
    ppermute x1, starting transfers between devices, per_device(): lax.ppermute(to_left, ('grp', 'tile'), [((i + 1) % tiles, i) for i in ran...  7.35 us
    pallas_call x1, Pallas kernels, edges(): pl.pallas_call(edges_kernel, grid=(levels // block,), in_specs=[pl.BlockS...  3.4 us
    ppermute x1, waiting for transfers between devices, per_device(): lax.ppermute(to_right, ('grp', 'tile'), [(i, (i + 1) % tiles) for i in ra...  2.33 us
    pallas_call x1, Pallas kernels, warm(): pl.pallas_call(warm_kernel, grid=(levels // block,), in_specs=[spec, pl.B...  2.09 us
    ppermute x1, starting transfers between devices, per_device(): lax.ppermute(to_right, ('grp', 'tile'), [(i, (i + 1) % tiles) for i in ra...  1.92 us
    ppermute x1, starting transfers between devices, per_device(): heat_in = lax.ppermute(heat, 'grp', [(1, 0)])  1.28 us
  transfers between devices with their start and end apart: 3, of which 2 were waited for; matrix products, arithmetic and copies ran while one was open for 0% of the time, Pallas kernels for 46%

profile of v4, /device:TPU:0, one launch (start us, length us, event | category | flops | bytes accessed | tf_op | source)
XLA Modules:
  0.0 35.2 jit_solution(15138066851094028759)
XLA Ops:
  0.0 0.0 copy-start
  0.0 0.0 copy-start.8
  0.0 0.0 copy-start.7
  0.0 0.0 copy-start.6
  0.0 0.0 copy-start.5
  0.0 0.0 copy-start.1
  0.0 0.0 copy-start.4
  0.0 0.0 copy-start.3
  0.0 0.0 copy-start.2
  0.1 3.4 %conditional.4 = ((f32[8,64,256]{2,1,0:T(8,128)S(1)}, f32[9,64,256]{2,1,0:T(8,128)S(1)})) conditional(s32[]{:T(128)} %convert_element_type.2, () %tuple.26, (f32[4,64,16,256]{3,2,1,0:T(8,128)}, f32[2,64,16,256]{3,2,1,0:T(8,128)}) %tuple.24), branch_computations={%region_2.0_spmd, %region_3.0_spmd} | conditional | bytes 8 | solution.py:462
  0.1 3.4 %edges.1 = (f32[8,64,256]{2,1,0:T(8,128)S(1)}, f32[9,64,256]{2,1,0:T(8,128)S(1)}) custom-call(f32[4,64,16,256]{3,2,1,0:T(8,128)} %get-tuple-element.66.prog_ref, f32[2,64,16,256]{3,2,1,0:T(8,128)} %get-tuple-element.67.cour_ref), custom_call_target="tpu_custom_call" | custom-call | tf_op jit(solution)/shard_map/cond/branch_1_fun/edges/pallas_call | solution.py:281
  3.5 7.4 %collective-permute-start.1 = (f32[9,64,256]{2,1,0:T(8,128)S(1)}, f32[9,64,256]{2,1,0:T(8,128)S(1)}, u32[]{:S(2)}, u32[]{:S(2)}) collective-permute-start(f32[9,64,256]{2,1,0:T(8,128)S(1)} %get-tuple-element.86), channel_id=1, source_target_pairs={{1,0},{2,1},{3,2},{4,3},{5,4},{6,5},{7,6},{8,7},{9,8},{10,9},{11,1... | collective-permute-start | bytes 1769480 | tf_op jit(solution)/shard_map/ppermute | solution.py:466
  10.8 1.9 %collective-permute-start = (f32[8,64,256]{2,1,0:T(8,128)S(1)}, f32[8,64,256]{2,1,0:T(8,128)S(1)}, u32[]{:S(2)}, u32[]{:S(2)}) collective-permute-start(f32[8,64,256]{2,1,0:T(8,128)S(1)} %get-tuple-element.85), channel_id=1, source_target_pairs={{0,1},{1,2},{2,3},{3,4},{4,5},{5,6},{6,7},{7,8},{8,9},{9,10},{10,1... | collective-permute-start | bytes 1572872 | tf_op jit(solution)/shard_map/ppermute | solution.py:465
  12.8 0.0 copy-done
  12.8 0.0 copy-done.8
  12.8 0.0 copy-done.7
  12.8 0.0 copy-done.6
  12.8 0.0 copy-done.5
  12.8 0.0 copy-done.1
  12.8 0.0 copy-done.4
  12.8 0.0 copy-done.3
  12.9 0.0 copy-done.2
  12.9 7.6 %conditional.3 = ((f32[4,64,16,256]{3,2,1,0:T(8,128)}, f32[64,8,128]{2,1,0:T(8,128)}, f32[4,64,8,128]{3,2,1,0:T(8,128)S(1)})) conditional(s32[]{:T(128)} %convert_element_type.2, (s32[1024]{0:T(1024)S(1)}, f32[1024]{0:T(1024)S(1)}, f32[1024]{0:T(1024)S(1)}, f32[64]{0:T(128)S(1)}, f32[64,32]{0,1:T(8,128)S(1)}, /*index=5*/f32[32]{0:T(128)S(1)}, ...), branch_computations={%region_0.0_spmd, %region_1.0_spmd} | conditional | bytes 16392 | solution.py:467
  12.9 7.5 %pass_one.1 = (f32[4,64,16,256]{3,2,1,0:T(8,128)}, f32[64,8,128]{2,1,0:T(8,128)}, f32[4,64,8,128]{3,2,1,0:T(8,128)S(1)}) custom-call(f32[4,64,16,256]{3,2,1,0:T(8,128)} %get-tuple-element.64.prog_ref, f32[2,64,16,256]{3,2,1,0:T(8,128)} %get-tuple-element.65.cour_ref), custom_call_target="tpu_custom_call" | custom-call | tf_op jit(solution)/shard_map/cond/branch_1_fun/pass_one/pallas_call | solution.py:345
  20.4 1.3 %collective-permute-start.2 = (f32[64,8,128]{2,1,0:T(8,128)}, f32[64,8,128]{2,1,0:T(8,128)S(1)}, u32[]{:S(2)}, u32[]{:S(2)}) collective-permute-start(f32[64,8,128]{2,1,0:T(8,128)} %get-tuple-element.82), channel_id=1, source_target_pairs={{16,0},{17,1},{18,2},{19,3},{20,4},{21,5},{22,6},{23,7},{24,8},{25... | collective-permute-start | bytes 786440 | tf_op jit(solution)/shard_map/ppermute | solution.py:472
  21.7 2.3 %collective-permute-done = f32[8,64,256]{2,1,0:T(8,128)S(1)} collective-permute-done((f32[8,64,256]{2,1,0:T(8,128)S(1)}, f32[8,64,256]{2,1,0:T(8,128)S(1)}, u32[]{:S(2)}, u32[]{:S(2)}) %collective-permute-start) | collective-permute-done | bytes 524320 | tf_op jit(solution)/shard_map/ppermute | solution.py:465
  24.0 0.0 collective-permute-done.1
  24.0 8.7 %conditional.5 = (f32[4,64,16,256]{3,2,1,0:T(8,128)}) conditional(s32[]{:T(128)} %convert_element_type.2, (s32[1024]{0:T(1024)S(1)}, f32[64,8,128]{2,1,0:T(8,128)}, f32[4,64,8,128]{3,2,1,0:T(8,128)S(1)}) %tuple.40, (f32[4,64,16,256]{3,2,1,0:T(8,128)}, f32[2,64,16,256]{3,2,1,0:T(8,128)}, f32[8,64,256]{2,1,0:T(8,128)S(1)}, f32[9,64,256]{2,1,0:T(8,128)S(1)}, ...), branch_computations={%region_4.0_spmd, %region_5.0_spmd} | conditional | bytes 8 | solution.py:473
  24.0 8.7 %pass_two.1 = f32[4,64,16,256]{3,2,1,0:T(8,128)} custom-call(f32[4,64,16,256]{3,2,1,0:T(8,128)} %get-tuple-element.71.first_ref, f32[2,64,16,256]{3,2,1,0:T(8,128)} %get-tuple-element.72.cour_ref, f32[8,64,256]{2,1,0:T(8,128)S(1)} %get-tuple-element.73.my_right, f32[9,64,256]{2,1,0:T(8,128)S(1)} %get-tuple-element.74.my_left, ...), custom_call_target="tpu_custom_call" | custom-call | tf_op jit(solution)/shard_map/cond/branch_1_fun/pass_two/pallas_call | solution.py:409
  32.8 0.4 %collective-permute-done.2.heat_ref = f32[64,8,128]{2,1,0:T(8,128)S(1)} collective-permute-done((f32[64,8,128]{2,1,0:T(8,128)}, f32[64,8,128]{2,1,0:T(8,128)S(1)}, u32[]{:S(2)}, u32[]{:S(2)}) %collective-permute-start.2) | collective-permute-done | bytes 262176 | tf_op jit(solution)/shard_map/ppermute | solution.py:472
  33.1 2.1 %warm.1 = f32[4,64,16,256]{3,2,1,0:T(8,128)} custom-call(f32[4,64,16,256]{3,2,1,0:T(8,128)} %get-tuple-element.125.field_ref, f32[64,8,128]{2,1,0:T(8,128)S(1)} %collective-permute-done.2.heat_ref), custom_call_target="tpu_custom_call", output_to_operand_aliasing={{}: (0, {})} | custom-call | tf_op jit(solution)/shard_map/warm/pallas_call | solution.py:447
Async XLA Ops:
  0.0 12.8 %copy-start = (s32[1024]{0:T(1024)S(1)}, s32[1024]{0:T(1024)}, u32[]{:S(2)}) copy-start(s32[1024]{0:T(1024)} %param.19) | copy-start | bytes 12292
  0.0 12.8 %copy-start.8 = (f32[32]{0:T(128)S(1)}, f32[32]{0:T(128)}, u32[]{:S(2)}) copy-start(f32[32]{0:T(128)} %param.27) | copy-start | bytes 388
  0.0 12.8 %copy-start.7 = (f32[32]{0:T(128)S(1)}, f32[32]{0:T(128)}, u32[]{:S(2)}) copy-start(f32[32]{0:T(128)} %param.26) | copy-start | bytes 388
  0.0 12.8 %copy-start.6 = (f32[32]{0:T(128)S(1)}, f32[32]{0:T(128)}, u32[]{:S(2)}) copy-start(f32[32]{0:T(128)} %param.25) | copy-start | bytes 388
  0.0 12.8 %copy-start.5 = (f32[32]{0:T(128)S(1)}, f32[32]{0:T(128)}, u32[]{:S(2)}) copy-start(f32[32]{0:T(128)} %param.24) | copy-start | bytes 388
  0.0 12.8 %copy-start.1 = (f32[64,32]{0,1:T(8,128)S(1)}, f32[64,32]{0,1:T(8,128)}, u32[]{:S(2)}) copy-start(f32[64,32]{0,1:T(8,128)} %param.23) | copy-start | bytes 24580
  0.0 12.8 %copy-start.4 = (f32[64]{0:T(128)S(1)}, f32[64]{0:T(128)}, u32[]{:S(2)}) copy-start(f32[64]{0:T(128)} %param.22) | copy-start | bytes 772
  0.0 12.8 %copy-start.3 = (f32[1024]{0:T(1024)S(1)}, f32[1024]{0:T(1024)}, u32[]{:S(2)}) copy-start(f32[1024]{0:T(1024)} %param.21) | copy-start | bytes 12292
  0.0 12.8 %copy-start.2 = (f32[1024]{0:T(1024)S(1)}, f32[1024]{0:T(1024)}, u32[]{:S(2)}) copy-start(f32[1024]{0:T(1024)} %param.20) | copy-start | bytes 12292
  3.5 20.6 %collective-permute-start.1 = (f32[9,64,256]{2,1,0:T(8,128)S(1)}, f32[9,64,256]{2,1,0:T(8,128)S(1)}, u32[]{:S(2)}, u32[]{:S(2)}) collective-permute-start(f32[9,64,256]{2,1,0:T(8,128)S(1)} %get-tuple-element.86), channel_id=1, source_target_pairs={{1,0},{2,1},{3,2},{4,3},{5,4},{6,5},{7,6},{8,7},{9,8},{10,9},{11,1... | collective-permute-start | bytes 1769480 | tf_op jit(solution)/shard_map/ppermute | solution.py:466
  10.8 13.2 %collective-permute-start = (f32[8,64,256]{2,1,0:T(8,128)S(1)}, f32[8,64,256]{2,1,0:T(8,128)S(1)}, u32[]{:S(2)}, u32[]{:S(2)}) collective-permute-start(f32[8,64,256]{2,1,0:T(8,128)S(1)} %get-tuple-element.85), channel_id=1, source_target_pairs={{0,1},{1,2},{2,3},{3,4},{4,5},{5,6},{6,7},{7,8},{8,9},{9,10},{10,1... | collective-permute-start | bytes 1572872 | tf_op jit(solution)/shard_map/ppermute | solution.py:465
  20.4 12.7 %collective-permute-start.2 = (f32[64,8,128]{2,1,0:T(8,128)}, f32[64,8,128]{2,1,0:T(8,128)S(1)}, u32[]{:S(2)}, u32[]{:S(2)}) collective-permute-start(f32[64,8,128]{2,1,0:T(8,128)} %get-tuple-element.82), channel_id=1, source_target_pairs={{16,0},{17,1},{18,2},{19,3},{20,4},{21,5},{22,6},{23,7},{24,8},{25... | collective-permute-start | bytes 786440 | tf_op jit(solution)/shard_map/ppermute | solution.py:472

commit v5 on v4

--- a/solution.py
+++ b/solution.py
@@ -12,12 +12,12 @@
 STEP_LENGTH = 1.0
 LOG2E = 1.4426950408889634
 G_CHUNK = 8
-UP_UNROLL = 4
+UP_UNROLL = 8
 DOWN_UNROLL = 4
 EDGE_BLOCK = 32
 ONE_BLOCK = 16
 ONE_UNROLL = 4
-TWO_BLOCK = 16
+TWO_BLOCK = 32
 TWO_UNROLL = 4
 EXPAND_BLOCK = 16
 WARM_BLOCK = 32

time: 35.6 us -> 35.7 us (level)
  Pallas kernels: 21.7 us -> 22.2 us
  waiting for transfers between devices: 2.7 us -> 2.34 us
    pallas_call x1, Pallas kernels: 8.72 us -> 9.19 us  [pass_two(): pl.pallas_call(pass_two_kernel, grid=(levels // block,), in_specs=[plane,...]
  transfers between devices with their start and end apart: 3 -> 3, of which waited for: 2 -> 1; matrix products, arithmetic and copies ran while one was open for 0% -> 0% of each run, Pallas kernels for 46% -> 47%
where the time goes in v5:
time: 35.7 us; the launch traced here: 35.3 us
  Pallas kernels  22.2 us (62%)
  starting transfers between devices  10.6 us (30%)
  waiting for transfers between devices  2.34 us (7%)
    pallas_call x1, Pallas kernels, pass_two(): pl.pallas_call(pass_two_kernel, grid=(levels // block,), in_specs=[plane,...  9.19 us
    pallas_call x1, Pallas kernels, pass_one(): pl.pallas_call(pass_one_kernel, grid=(levels // block,), in_specs=[plane,...  7.54 us
    ppermute x1, starting transfers between devices, per_device(): lax.ppermute(to_left, ('grp', 'tile'), [((i + 1) % tiles, i) for i in ran...  7.35 us
    pallas_call x1, Pallas kernels, edges(): pl.pallas_call(edges_kernel, grid=(levels // block,), in_specs=[pl.BlockS...  3.4 us
    ppermute x1, waiting for transfers between devices, per_device(): lax.ppermute(to_right, ('grp', 'tile'), [(i, (i + 1) % tiles) for i in ra...  2.33 us
    pallas_call x1, Pallas kernels, warm(): pl.pallas_call(warm_kernel, grid=(levels // block,), in_specs=[spec, pl.B...  2.1 us
    ppermute x1, starting transfers between devices, per_device(): lax.ppermute(to_right, ('grp', 'tile'), [(i, (i + 1) % tiles) for i in ra...  1.92 us
    ppermute x1, starting transfers between devices, per_device(): heat_in = lax.ppermute(heat, 'grp', [(1, 0)])  1.28 us
  transfers between devices with their start and end apart: 3, of which 1 were waited for; matrix products, arithmetic and copies ran while one was open for 0% of the time, Pallas kernels for 47%

profile of v5, /device:TPU:0, one launch (start us, length us, event | category | flops | bytes accessed | tf_op | source)
XLA Modules:
  0.0 35.3 jit_solution(11732599325292330304)
XLA Ops:
  0.0 0.0 copy-start
  0.0 0.0 copy-start.8
  0.0 0.0 copy-start.7
  0.0 0.0 copy-start.6
  0.0 0.0 copy-start.5
  0.0 0.0 copy-start.1
  0.0 0.0 copy-start.4
  0.0 0.0 copy-start.3
  0.0 0.0 copy-start.2
  0.1 3.4 %conditional.4 = ((f32[8,64,256]{2,1,0:T(8,128)S(1)}, f32[9,64,256]{2,1,0:T(8,128)S(1)})) conditional(s32[]{:T(128)} %convert_element_type.2, () %tuple.26, (f32[4,64,16,256]{3,2,1,0:T(8,128)}, f32[2,64,16,256]{3,2,1,0:T(8,128)}) %tuple.24), branch_computations={%region_2.0_spmd, %region_3.0_spmd} | conditional | bytes 8 | solution.py:462
  0.1 3.4 %edges.1 = (f32[8,64,256]{2,1,0:T(8,128)S(1)}, f32[9,64,256]{2,1,0:T(8,128)S(1)}) custom-call(f32[4,64,16,256]{3,2,1,0:T(8,128)} %get-tuple-element.66.prog_ref, f32[2,64,16,256]{3,2,1,0:T(8,128)} %get-tuple-element.67.cour_ref), custom_call_target="tpu_custom_call" | custom-call | tf_op jit(solution)/shard_map/cond/branch_1_fun/edges/pallas_call | solution.py:281
  3.5 7.4 %collective-permute-start.1 = (f32[9,64,256]{2,1,0:T(8,128)S(1)}, f32[9,64,256]{2,1,0:T(8,128)S(1)}, u32[]{:S(2)}, u32[]{:S(2)}) collective-permute-start(f32[9,64,256]{2,1,0:T(8,128)S(1)} %get-tuple-element.86), channel_id=1, source_target_pairs={{1,0},{2,1},{3,2},{4,3},{5,4},{6,5},{7,6},{8,7},{9,8},{10,9},{11,1... | collective-permute-start | bytes 1769480 | tf_op jit(solution)/shard_map/ppermute | solution.py:466
  10.8 1.9 %collective-permute-start = (f32[8,64,256]{2,1,0:T(8,128)S(1)}, f32[8,64,256]{2,1,0:T(8,128)S(1)}, u32[]{:S(2)}, u32[]{:S(2)}) collective-permute-start(f32[8,64,256]{2,1,0:T(8,128)S(1)} %get-tuple-element.85), channel_id=1, source_target_pairs={{0,1},{1,2},{2,3},{3,4},{4,5},{5,6},{6,7},{7,8},{8,9},{9,10},{10,1... | collective-permute-start | bytes 1572872 | tf_op jit(solution)/shard_map/ppermute | solution.py:465
  12.8 0.0 copy-done
  12.8 0.0 copy-done.8
  12.8 0.0 copy-done.7
  12.8 0.0 copy-done.6
  12.8 0.0 copy-done.5
  12.8 0.0 copy-done.1
  12.8 0.0 copy-done.4
  12.8 0.0 copy-done.3
  12.9 0.0 copy-done.2
  12.9 7.6 %conditional.3 = ((f32[4,64,16,256]{3,2,1,0:T(8,128)}, f32[64,8,128]{2,1,0:T(8,128)}, f32[4,64,8,128]{3,2,1,0:T(8,128)S(1)})) conditional(s32[]{:T(128)} %convert_element_type.2, (s32[1024]{0:T(1024)S(1)}, f32[1024]{0:T(1024)S(1)}, f32[1024]{0:T(1024)S(1)}, f32[64]{0:T(128)S(1)}, f32[64,32]{0,1:T(8,128)S(1)}, /*index=5*/f32[32]{0:T(128)S(1)}, ...), branch_computations={%region_0.0_spmd, %region_1.0_spmd} | conditional | bytes 16392 | solution.py:467
  12.9 7.5 %pass_one.1 = (f32[4,64,16,256]{3,2,1,0:T(8,128)}, f32[64,8,128]{2,1,0:T(8,128)}, f32[4,64,8,128]{3,2,1,0:T(8,128)S(1)}) custom-call(f32[4,64,16,256]{3,2,1,0:T(8,128)} %get-tuple-element.64.prog_ref, f32[2,64,16,256]{3,2,1,0:T(8,128)} %get-tuple-element.65.cour_ref), custom_call_target="tpu_custom_call" | custom-call | tf_op jit(solution)/shard_map/cond/branch_1_fun/pass_one/pallas_call | solution.py:345
  20.4 1.3 %collective-permute-start.2 = (f32[64,8,128]{2,1,0:T(8,128)}, f32[64,8,128]{2,1,0:T(8,128)S(1)}, u32[]{:S(2)}, u32[]{:S(2)}) collective-permute-start(f32[64,8,128]{2,1,0:T(8,128)} %get-tuple-element.82), channel_id=1, source_target_pairs={{16,0},{17,1},{18,2},{19,3},{20,4},{21,5},{22,6},{23,7},{24,8},{25... | collective-permute-start | bytes 786440 | tf_op jit(solution)/shard_map/ppermute | solution.py:472
  21.7 2.3 %collective-permute-done = f32[8,64,256]{2,1,0:T(8,128)S(1)} collective-permute-done((f32[8,64,256]{2,1,0:T(8,128)S(1)}, f32[8,64,256]{2,1,0:T(8,128)S(1)}, u32[]{:S(2)}, u32[]{:S(2)}) %collective-permute-start) | collective-permute-done | bytes 524320 | tf_op jit(solution)/shard_map/ppermute | solution.py:465
  24.0 0.0 collective-permute-done.1
  24.0 9.2 %conditional.5 = (f32[4,64,16,256]{3,2,1,0:T(8,128)}) conditional(s32[]{:T(128)} %convert_element_type.2, (s32[1024]{0:T(1024)S(1)}, f32[64,8,128]{2,1,0:T(8,128)}, f32[4,64,8,128]{3,2,1,0:T(8,128)S(1)}) %tuple.40, (f32[4,64,16,256]{3,2,1,0:T(8,128)}, f32[2,64,16,256]{3,2,1,0:T(8,128)}, f32[8,64,256]{2,1,0:T(8,128)S(1)}, f32[9,64,256]{2,1,0:T(8,128)S(1)}, ...), branch_computations={%region_4.0_spmd, %region_5.0_spmd} | conditional | bytes 8 | solution.py:473
  24.0 9.2 %pass_two.1 = f32[4,64,16,256]{3,2,1,0:T(8,128)} custom-call(f32[4,64,16,256]{3,2,1,0:T(8,128)} %get-tuple-element.71.first_ref, f32[2,64,16,256]{3,2,1,0:T(8,128)} %get-tuple-element.72.cour_ref, f32[8,64,256]{2,1,0:T(8,128)S(1)} %get-tuple-element.73.my_right, f32[9,64,256]{2,1,0:T(8,128)S(1)} %get-tuple-element.74.my_left, ...), custom_call_target="tpu_custom_call" | custom-call | tf_op jit(solution)/shard_map/cond/branch_1_fun/pass_two/pallas_call | solution.py:409
  33.2 0.0 collective-permute-done.2.heat_ref
  33.2 2.1 %warm.1 = f32[4,64,16,256]{3,2,1,0:T(8,128)} custom-call(f32[4,64,16,256]{3,2,1,0:T(8,128)} %get-tuple-element.125.field_ref, f32[64,8,128]{2,1,0:T(8,128)S(1)} %collective-permute-done.2.heat_ref), custom_call_target="tpu_custom_call", output_to_operand_aliasing={{}: (0, {})} | custom-call | tf_op jit(solution)/shard_map/warm/pallas_call | solution.py:447
Async XLA Ops:
  0.0 12.8 %copy-start = (s32[1024]{0:T(1024)S(1)}, s32[1024]{0:T(1024)}, u32[]{:S(2)}) copy-start(s32[1024]{0:T(1024)} %param.19) | copy-start | bytes 12292
  0.0 12.8 %copy-start.8 = (f32[32]{0:T(128)S(1)}, f32[32]{0:T(128)}, u32[]{:S(2)}) copy-start(f32[32]{0:T(128)} %param.27) | copy-start | bytes 388
  0.0 12.8 %copy-start.7 = (f32[32]{0:T(128)S(1)}, f32[32]{0:T(128)}, u32[]{:S(2)}) copy-start(f32[32]{0:T(128)} %param.26) | copy-start | bytes 388
  0.0 12.8 %copy-start.6 = (f32[32]{0:T(128)S(1)}, f32[32]{0:T(128)}, u32[]{:S(2)}) copy-start(f32[32]{0:T(128)} %param.25) | copy-start | bytes 388
  0.0 12.8 %copy-start.5 = (f32[32]{0:T(128)S(1)}, f32[32]{0:T(128)}, u32[]{:S(2)}) copy-start(f32[32]{0:T(128)} %param.24) | copy-start | bytes 388
  0.0 12.8 %copy-start.1 = (f32[64,32]{0,1:T(8,128)S(1)}, f32[64,32]{0,1:T(8,128)}, u32[]{:S(2)}) copy-start(f32[64,32]{0,1:T(8,128)} %param.23) | copy-start | bytes 24580
  0.0 12.8 %copy-start.4 = (f32[64]{0:T(128)S(1)}, f32[64]{0:T(128)}, u32[]{:S(2)}) copy-start(f32[64]{0:T(128)} %param.22) | copy-start | bytes 772
  0.0 12.8 %copy-start.3 = (f32[1024]{0:T(1024)S(1)}, f32[1024]{0:T(1024)}, u32[]{:S(2)}) copy-start(f32[1024]{0:T(1024)} %param.21) | copy-start | bytes 12292
  0.0 12.8 %copy-start.2 = (f32[1024]{0:T(1024)S(1)}, f32[1024]{0:T(1024)}, u32[]{:S(2)}) copy-start(f32[1024]{0:T(1024)} %param.20) | copy-start | bytes 12292
  3.5 20.6 %collective-permute-start.1 = (f32[9,64,256]{2,1,0:T(8,128)S(1)}, f32[9,64,256]{2,1,0:T(8,128)S(1)}, u32[]{:S(2)}, u32[]{:S(2)}) collective-permute-start(f32[9,64,256]{2,1,0:T(8,128)S(1)} %get-tuple-element.86), channel_id=1, source_target_pairs={{1,0},{2,1},{3,2},{4,3},{5,4},{6,5},{7,6},{8,7},{9,8},{10,9},{11,1... | collective-permute-start | bytes 1769480 | tf_op jit(solution)/shard_map/ppermute | solution.py:466
  10.8 13.2 %collective-permute-start = (f32[8,64,256]{2,1,0:T(8,128)S(1)}, f32[8,64,256]{2,1,0:T(8,128)S(1)}, u32[]{:S(2)}, u32[]{:S(2)}) collective-permute-start(f32[8,64,256]{2,1,0:T(8,128)S(1)} %get-tuple-element.85), channel_id=1, source_target_pairs={{0,1},{1,2},{2,3},{3,4},{4,5},{5,6},{6,7},{7,8},{8,9},{9,10},{10,1... | collective-permute-start | bytes 1572872 | tf_op jit(solution)/shard_map/ppermute | solution.py:465
  20.4 12.8 %collective-permute-start.2 = (f32[64,8,128]{2,1,0:T(8,128)}, f32[64,8,128]{2,1,0:T(8,128)S(1)}, u32[]{:S(2)}, u32[]{:S(2)}) collective-permute-start(f32[64,8,128]{2,1,0:T(8,128)} %get-tuple-element.82), channel_id=1, source_target_pairs={{16,0},{17,1},{18,2},{19,3},{20,4},{21,5},{22,6},{23,7},{24,8},{25... | collective-permute-start | bytes 786440 | tf_op jit(solution)/shard_map/ppermute | solution.py:472
